TPU v7x, 256 devices: a whole 4x4x8 slice. The times are simulated.
256 devices in a mesh: site: 16 (over y, z_lo), cuts: 16 (over z_hi, x, core).
Axes of the slice: x: 4, y: 4, z: 8 (z_hi: 2, z_lo: 4; z = z_hi * 4 + z_lo), core: 2. Of those that a mesh axis runs over, the one named last changes fastest.
Arguments:
- eigen_vectors: bfloat16 [32, 2, 3, 256, 9216], P('cuts', None, None, None, 'site'), may hold values from -6 to 6
- perambulators: bfloat16 [512, 2, 1024, 512], P(('site', 'cuts')), may hold values from -0.049804688 to 0.049804688
- momenta: int32 [3, 3], replicated, may hold values from 1 to 3
- source_slice: int32 [1], replicated, may hold values from 0 to 31
- sink_slices: int32 [512], P(('site', 'cuts')), may hold values from 0 to 1
- sink_momenta: int32 [512], P(('site', 'cuts')), may hold values from 0 to 2
- spin_order: int32 [4], replicated, may hold values from 0 to 3, each once
Outputs:
- correlators: bfloat16 [512, 2, 512, 512], P(('site', 'cuts'))
Inputs may be any that keep to these rules, and one draw needn't show every extreme that they name: `spin_order`: a permutation of 0 to 3.
All inputs are finite; a program needn't handle non-finite values.
Results may differ from a plain program's by a relative error of at most 0.0081.
Values may be sent and summed in bfloat16 or wider, within the bound.
No kernel may reach another device: no remote copies, remote signals or barrier semaphores. Data moves between devices by JAX's collectives and lax.ppermute only.
A program may use at most 64 MiB of HBM per device.

v0:
```python
import functools
import math

import jax
import jax.numpy as jnp
from jax import lax
from jax.experimental import pallas as pl
from jax.experimental.pallas import tpu as pltpu
from jax.sharding import PartitionSpec as P


L = 96
PLANES = 1
NMOM = 3
NVEC = 256
YN = 4
ZN = 4
SCALE = 1.0 / math.sqrt(6.0 * L * L * PLANES)
F32 = jnp.float32
BF16 = jnp.bfloat16


def y_swap(step):
    return [(y * ZN + z, (y ^ step) * ZN + z) for y in range(YN) for z in range(ZN)]


def z_swap(step):
    return [(y * ZN + z, y * ZN + (z ^ step)) for y in range(YN) for z in range(ZN)]


def cut_swap(dx, dc):
    return [
        (h * 8 + x * 2 + c, h * 8 + (x ^ dx) * 2 + (c ^ dc))
        for h in range(2)
        for x in range(4)
        for c in range(2)
    ]


def half_swap():
    return [
        ((y * ZN + z) * 16 + h * 8 + rest, (y * ZN + (z ^ 2)) * 16 + (h ^ 1) * 8 + rest)
        for y in range(YN)
        for z in range(ZN)
        for h in range(2)
        for rest in range(8)
    ]


def sin_cos(winding):
    quarter = jnp.floor((winding + 12.5) * (1.0 / 24.0))
    angle = (winding - 24.0 * quarter) * (2.0 * math.pi / L)
    sq = angle * angle
    sine = angle * (1.0 + sq * (-1 / 6 + sq * (1 / 120 + sq * (-1 / 5040 + sq * (1 / 362880)))))
    cosine = 1.0 + sq * (
        -1 / 2 + sq * (1 / 24 + sq * (-1 / 720 + sq * (1 / 40320 + sq * (-1 / 3628800))))
    )
    odd = (quarter == 1.0) | (quarter == 3.0)
    cos_out = jnp.where(odd, sine, cosine)
    sin_out = jnp.where(odd, cosine, sine)
    cos_out = jnp.where((quarter == 1.0) | (quarter == 2.0), -cos_out, cos_out)
    sin_out = jnp.where((quarter == 2.0) | (quarter == 3.0), -sin_out, sin_out)
    return cos_out, sin_out


def scalar_row(source, turned):
    near = source[0] % 2
    return near, (1 - near if turned else near)


def elementals_kernel(
    turned, source, mom, slices, moments, v_hbm, keep, send1, send2, send3, acc, trig, wide_trig, flipped, phased, vbuf, kbuf, sbuf, sems
):
    depth = vbuf.shape[1]
    count = depth // 3
    padded = flipped.shape[1]
    span = trig.shape[1]
    near, mine = scalar_row(source, turned)
    place = lax.axis_index("site")
    my_y = place // ZN
    loads = []
    for colour in range(3):
        rows = pl.ds(colour * count, count)
        load = pltpu.make_async_copy(
            v_hbm.at[mine, :, rows, :], vbuf.at[:, rows, :], sems.at[colour]
        )
        load.start()
        loads.append(load)
    site = (place * count + lax.broadcasted_iota(jnp.int32, (1, span), 1)).astype(F32)
    row = jnp.floor((site + 0.5) * (1.0 / L))
    x = site - L * row
    z = jnp.floor((row + 0.5) * (1.0 / L))
    y = row - L * z
    for p in range(NMOM):
        turn = (
            mom[p, 0].astype(F32) * x + mom[p, 1].astype(F32) * y + mom[p, 2].astype(F32) * z
        )
        turn = turn - L * jnp.floor((turn + 0.5) * (1.0 / L))
        cosine, sine = sin_cos(turn)
        trig[p : p + 1, :] = cosine
        trig[p + NMOM : p + NMOM + 1, :] = sine
    columns = trig[...].T
    for q in range(2 * NMOM):
        wide_trig[q] = jnp.broadcast_to(columns[:count, q : q + 1], (count, 128))
    phased[depth:, :] = jnp.zeros((padded - depth, 2 * NVEC), BF16)
    waited = 0
    for first in range(0, padded, 128):
        rows = min(128, depth - first)
        while waited < 3 and first + rows > waited * count:
            loads[waited].wait()
            waited += 1
        for part in range(2):
            block = vbuf[part, first : first + rows, :]
            if rows < 128:
                block = jnp.concatenate([block, jnp.zeros((128 - rows, NVEC), BF16)], axis=0)
            flipped[part * NVEC : (part + 1) * NVEC, first : first + 128] = block.T
    for p in range(NMOM):
        for colour in range(3):
            rows = slice(colour * count, (colour + 1) * count)
            for half in range(2):
                cols = slice(half * 128, (half + 1) * 128)
                real = vbuf[0, rows, cols].astype(F32)
                imag = vbuf[1, rows, cols].astype(F32)
                cosine = wide_trig[p]
                sine = wide_trig[p + NMOM]
                phased[rows, half * 128 : half * 128 + 128] = (cosine * real + sine * imag).astype(BF16)
                phased[rows, NVEC + half * 128 : NVEC + half * 128 + 128] = (
                    cosine * imag - sine * real
                ).astype(BF16)
        product = jnp.dot(flipped[...], phased[...], preferred_element_type=F32)
        acc[2 * p] = product[:NVEC, :NVEC] + product[NVEC:, NVEC:]
        acc[2 * p + 1] = product[:NVEC, NVEC:] - product[NVEC:, :NVEC]
    rows = NVEC // YN
    at_row = lax.broadcasted_iota(jnp.int32, (16, NVEC), 0)
    flat = [moments[k] + NMOM * (slices[k] != near).astype(jnp.int32) for k in range(2)]
    note = jnp.where(at_row == 0, flat[0], flat[1]).astype(F32).astype(BF16)
    stores = []
    for step in (2, 1, 3, 0):
        first = pl.multiple_of((my_y ^ step) * rows, rows)
        buf, out = (kbuf, keep) if step == 0 else (sbuf.at[step - 1], (send1, send2, send3)[step - 1])
        for r in range(2 * NMOM):
            buf[r * rows : (r + 1) * rows, :] = (acc[r, pl.ds(first, rows), :] * SCALE).astype(buf.dtype)
        if step:
            buf[2 * NMOM * rows :, :] = note
        store = pltpu.make_async_copy(buf, out, sems.at[3 + step])
        store.start()
        stores.append(store)
    for store in stores:
        store.wait()


def partial_elementals(turned, source, momenta, slices, moments, vectors):
    depth = vectors.shape[2]
    count = depth // 3
    padded = -(-depth // 256) * 256
    height = 2 * NMOM * NVEC // YN
    hbm = lambda: pl.BlockSpec(memory_space=pltpu.HBM)
    sent = jax.ShapeDtypeStruct((height + 16, NVEC), BF16)
    smem = lambda: pl.BlockSpec(memory_space=pltpu.SMEM)
    return pl.pallas_call(
        functools.partial(elementals_kernel, turned),
        in_specs=[smem(), smem(), smem(), smem(), hbm()],
        out_specs=[hbm(), hbm(), hbm(), hbm()],
        scratch_shapes=[
            pltpu.VMEM((2 * NMOM, NVEC, NVEC), F32),
            pltpu.VMEM((8, -(-count // 128) * 128), F32),
            pltpu.VMEM((2 * NMOM, count, 128), F32),
            pltpu.VMEM((2 * NVEC, padded), BF16),
            pltpu.VMEM((padded, 2 * NVEC), BF16),
            pltpu.VMEM((2, depth, NVEC), BF16),
            pltpu.VMEM((height, NVEC), F32),
            pltpu.VMEM((3, height + 16, NVEC), BF16),
            pltpu.SemaphoreType.DMA((7,)),
        ],
        out_shape=[jax.ShapeDtypeStruct((height, NVEC), F32), sent, sent, sent],
        compiler_params=pltpu.CompilerParams(vmem_limit_bytes=60 * 1024 * 1024),
        name="elementals",
    )(source, momenta, slices, moments, vectors)


def sum_kernel(kept, got1, got2, got3, keep, send1, send2, send3):
    rows = NVEC // YN // ZN
    for step, out in enumerate((keep, send1, send2, send3)):
        for r in range(2 * NMOM):
            first = pl.multiple_of(r * NVEC // YN + (lax.axis_index("site") % ZN ^ step) * rows, rows)
            part = kept[pl.ds(first, rows), :]
            for got in (got1, got2, got3):
                part = part + got[pl.ds(first, rows), :].astype(F32)
            out[r * rows : (r + 1) * rows, :] = part.astype(out.dtype)


def sum_and_split(kept, got):
    height = 2 * NMOM * NVEC // YN // ZN
    piece = lambda dtype: jax.ShapeDtypeStruct((height, NVEC), dtype)
    vmem = lambda: pl.BlockSpec(memory_space=pltpu.VMEM)
    return pl.pallas_call(
        sum_kernel,
        in_specs=[vmem() for _ in range(4)],
        out_specs=[vmem() for _ in range(4)],
        out_shape=[piece(F32), piece(BF16), piece(BF16), piece(BF16)],
        compiler_params=pltpu.CompilerParams(vmem_limit_bytes=6 << 20),
        name="sum_split",
    )(kept, *got)


def flip_kernel(t_ref, out):
    for part in range(2):
        out[0, :, part * NVEC : (part + 1) * NVEC] = t_ref[0, part, 0].T


def transposed(perams):
    count, _, spins, nvec, columns = perams.shape
    return pl.pallas_call(
        flip_kernel,
        grid=(count, spins),
        in_specs=[pl.BlockSpec((1, 2, 1, nvec, columns), lambda k, s: (k, 0, s, 0, 0))],
        out_specs=pl.BlockSpec((1, columns, 2 * nvec), lambda k, s: (k, 0, s)),
        out_shape=jax.ShapeDtypeStruct((count, columns, spins * 2 * nvec), BF16),
        compiler_params=pltpu.CompilerParams(vmem_limit_bytes=8 << 20),
        name="transpose_tau",
    )(perams)


def pick_kernel(idx, p0, p1, p2, p3, *outs):
    for step, out in enumerate(outs):
        for k in range(2):
            for dz, piece in enumerate((p0, p1, p2, p3)):
                out[k, dz] = piece[idx[step, k]]


def pick(idx, pieces):
    rows = NVEC // YN // ZN
    vmem = lambda: pl.BlockSpec(memory_space=pltpu.VMEM)
    piece = jax.ShapeDtypeStruct((2, ZN, 2, rows, NVEC), BF16)
    return pl.pallas_call(
        pick_kernel,
        in_specs=[pl.BlockSpec(memory_space=pltpu.SMEM)] + [vmem() for _ in pieces],
        out_specs=[vmem() for _ in range(4)],
        out_shape=[piece] * 4,
        compiler_params=pltpu.CompilerParams(vmem_limit_bytes=6 << 20),
    )(idx, *pieces)


def first_row(y, z, dy, dz):
    rows = NVEC // YN // ZN
    return pl.multiple_of((y ^ dy) * (ZN * rows) + (z ^ dz) * rows, rows)


def middle_kernel(source, f0, f1, f2, f3, t_ref, tt_ref, out, fmat, gmat):
    k = pl.program_id(0)
    rows = NVEC // YN // ZN
    site = lax.axis_index("site")
    same_half = lax.axis_index("cuts") // 8 == source[0] // 2 // 8
    my_y = site // ZN
    my_z = site % ZN
    far_z = my_z ^ jnp.where(same_half, 0, 2)
    for dy, f_ref in enumerate((f0, f1, f2, f3)):
        for dz in range(ZN):
            first = first_row(my_y, far_z, dy, dz)
            f_re = f_ref[k, dz, 0]
            f_im = f_ref[k, dz, 1]
            fmat[pl.ds(first, rows), :NVEC] = f_re
            fmat[pl.ds(first, rows), NVEC:] = -f_im
            fmat[pl.ds(NVEC + first, rows), :NVEC] = f_im
            fmat[pl.ds(NVEC + first, rows), NVEC:] = f_re
    wide = t_ref.shape[-1]
    f_all = fmat[...]
    for spin in range(4):
        tau = t_ref[0, :, spin].reshape(2 * NVEC, wide)
        left = jnp.dot(f_all, tau, preferred_element_type=F32).astype(BF16)
        home = (spin + 2) % 4
        if home >= 2:
            left = -left
        base = home * 2 * NVEC
        gmat[base : base + NVEC, :wide] = left[:NVEC]
        gmat[base + NVEC : base + 2 * NVEC, :wide] = left[NVEC:]
        gmat[base : base + NVEC, wide:] = left[NVEC:]
        gmat[base + NVEC : base + 2 * NVEC, wide:] = -left[:NVEC]
    out[0] = jnp.dot(tt_ref[0], gmat[...], preferred_element_type=F32).astype(BF16)


def middle_of(source_slice, source, perams, perams_t):
    count, _, spins, nvec, wide = perams.shape
    rows = NVEC // YN // ZN
    f_spec = lambda: pl.BlockSpec((count, ZN, 2, rows, NVEC), lambda k, *_: (0, 0, 0, 0, 0))
    return pl.pallas_call(
        middle_kernel,
        grid_spec=pltpu.PrefetchScalarGridSpec(
            num_scalar_prefetch=1,
            grid=(count,),
            in_specs=[f_spec() for _ in range(4)]
            + [
                pl.BlockSpec((1, 2, spins, nvec, wide), lambda k, *_: (k, 0, 0, 0, 0)),
                pl.BlockSpec((1, wide, spins * 2 * nvec), lambda k, *_: (k, 0, 0)),
            ],
            out_specs=pl.BlockSpec((1, wide, 2 * wide), lambda k, *_: (k, 0, 0)),
            scratch_shapes=[
                pltpu.VMEM((2 * NVEC, 2 * NVEC), BF16),
                pltpu.VMEM((spins * 2 * nvec, 2 * wide), BF16),
            ],
        ),
        out_shape=jax.ShapeDtypeStruct((count, wide, 2 * wide), BF16),
        compiler_params=pltpu.CompilerParams(vmem_limit_bytes=36 << 20),
        name="middle",
    )(source_slice, *source, perams, perams_t)


def table_at(row, column):
    shared = row & column
    return jnp.where(((shared & 1) ^ (shared >> 1)) == 1, -0.5, 0.5)


def outer_kernel(order, s0, s1, s2, s3, m_ref, out, smat):
    k = pl.program_id(0)
    rows = NVEC // YN // ZN
    site = lax.axis_index("site")
    my_y = site // ZN
    my_z = site % ZN
    for dy, s_ref in enumerate((s0, s1, s2, s3)):
        for dz in range(ZN):
            first = first_row(my_y, my_z, dy, dz)
            s_re = s_ref[k, dz, 0]
            s_im = s_ref[k, dz, 1]
            smat[pl.ds(first, rows), :NVEC] = s_re
            smat[pl.ds(first, rows), NVEC:] = s_im
            smat[pl.ds(NVEC + first, rows), :NVEC] = -s_im
            smat[pl.ds(NVEC + first, rows), NVEC:] = s_re
    wide = m_ref.shape[1]
    s_all = smat[...]
    inner = []
    for e in range(2):
        block = jnp.concatenate(
            [
                m_ref[0, :, e * NVEC : (e + 1) * NVEC],
                m_ref[0, :, wide + e * NVEC : wide + (e + 1) * NVEC],
            ],
            axis=1,
        )
        inner.append(jnp.dot(block, s_all, preferred_element_type=F32))
    for f in range(2):
        mixed = inner[0] * table_at(order[0], order[f]) + inner[1] * table_at(order[1], order[f])
        out[0, 0, :, f * NVEC : (f + 1) * NVEC] = mixed[:, :NVEC].astype(BF16)
        out[0, 1, :, f * NVEC : (f + 1) * NVEC] = mixed[:, NVEC:].astype(BF16)


def correlators_of(spin_order, sinks, middle):
    count, wide, _ = middle.shape
    rows = NVEC // YN // ZN
    s_spec = lambda: pl.BlockSpec((count, ZN, 2, rows, NVEC), lambda k, *_: (0, 0, 0, 0, 0))
    return pl.pallas_call(
        outer_kernel,
        grid_spec=pltpu.PrefetchScalarGridSpec(
            num_scalar_prefetch=1,
            grid=(count,),
            in_specs=[s_spec() for _ in range(4)]
            + [pl.BlockSpec((1, wide, 2 * wide), lambda k, *_: (k, 0, 0))],
            out_specs=pl.BlockSpec((1, 2, wide, wide), lambda k, *_: (k, 0, 0, 0)),
            scratch_shapes=[pltpu.VMEM((2 * NVEC, 2 * NVEC), BF16)],
        ),
        out_shape=jax.ShapeDtypeStruct((count, 2, wide, wide), BF16),
        compiler_params=pltpu.CompilerParams(vmem_limit_bytes=16 << 20),
        name="outer",
    )(spin_order, *sinks, middle)


def body(
    eigen_vectors, perambulators, momenta, source_slice, sink_slices, sink_momenta, spin_order
):
    slab_slices = eigen_vectors.shape[0]
    site_count = eigen_vectors.shape[-1]
    cut = lax.axis_index("cuts")
    source = source_slice[0]
    root = source // slab_slices
    near = source % slab_slices
    root_h = root // 8
    root_x = root // 2 % 4
    flat = (sink_slices != near).astype(jnp.int32) * NMOM + sink_momenta
    vectors = eigen_vectors.swapaxes(3, 4).reshape(slab_slices, 2, 3 * site_count, NVEC)

    def swap_y(parts):
        got = {}
        for step in (2, 1, 3):
            got[step] = lax.ppermute(parts[step], "site", y_swap(step))
        return [got[1], got[2], got[3]]

    def swap_z(parts):
        return [lax.ppermute(parts[step], "site", z_swap(step)) for step in (1, 2, 3)]

    def reduce_slice(turned):
        parts = partial_elementals(
            turned, source_slice, momenta, sink_slices, sink_momenta, vectors
        )
        got = swap_y(parts)
        notes = got
        parts = sum_and_split(parts[0], got)
        got = swap_z(parts)
        chunk = (parts[0] + sum(g.astype(F32) for g in got)).astype(BF16)
        return chunk.reshape(NMOM, 2, NVEC // YN // ZN, NVEC), notes

    chunk_a, notes = reduce_slice(False)
    chunk_b, _ = reduce_slice(True)
    tall = 2 * NMOM * NVEC // YN
    idx = jnp.stack([flat] + [v[tall : tall + 2, 0].astype(jnp.int32) for v in notes])

    held = chunk_a
    my_x = cut // 2 % 4
    for step in (1, 2, 3):
        got = lax.ppermute(chunk_a, "cuts", cut_swap(step, 0))
        held = jnp.where((my_x ^ step) == root_x, got, held)
    got = lax.ppermute(held, ("site", "cuts"), half_swap())
    held = jnp.where(cut // 8 == root_h, held, got)
    got = lax.ppermute(held, "cuts", cut_swap(0, 1))
    held = jnp.where(cut % 2 == root % 2, held, got)

    pieces = [held] + swap_z([held] * 4)
    parts = pick(idx % NMOM, pieces)
    source_parts = [parts[0]] + swap_y(parts)
    own_ab = jnp.concatenate([chunk_a, chunk_b], axis=0)
    pieces = [own_ab] + swap_z([own_ab] * 4)
    pieces, _ = lax.optimization_barrier((pieces, parts))
    parts = pick(idx, pieces)
    sink_parts = [parts[0]] + swap_y(parts)

    count = perambulators.shape[0]
    perams = perambulators.reshape(count, 2, 4, NVEC, 2 * NVEC)
    perams_t = transposed(perams)
    middle = middle_of(source_slice, source_parts, perams, perams_t)
    return correlators_of(spin_order, sink_parts, middle)


def solution(mesh):
    placed = (
        P("cuts", None, None, None, "site"),
        P(("site", "cuts"), None, None, None),
        P(),
        P(),
        P(("site", "cuts")),
        P(("site", "cuts")),
        P(),
    )
    return jax.shard_map(
        body,
        mesh=mesh,
        in_specs=placed,
        out_specs=P(("site", "cuts"), None, None, None),
        check_vma=False,
    )
```

profile of v0, /device:TPU:32, one launch (start us, length us, event | category | flops | bytes accessed | tf_op | source)
XLA Modules:
  0.0 98.6 jit_solution(6264363578741769389)
XLA Ops:
  0.7 7.1 %elementals.2 = (f32[384,256]{1,0:T(8,128)}, bf16[400,256]{1,0:T(8,128)(2,1)}, bf16[400,256]{1,0:T(8,128)(2,1)}, bf16[400,256]{1,0:T(8,128)(2,1)}) custom-call(s32[1]{0:T(128)} %copy.8.source, s32[3,3]{1,0:T(4,128)} %mom.3, s32[2]{0:T(128)} %slices.3, s32[2]{0:T(128)} %moments.3, bf16[2,2,1728,256]{3,2,1,0:T(8,128)(2,1)} %bitcast.18), custom_call_target="tpu_custom_call" | custom-call | tf_op jit(solution)/shard_map/elementals/pallas_call | solution.py:160
  7.8 1.7 %collective-permute-start = (bf16[400,256]{1,0:T(8,128)(2,1)}, bf16[400,256]{1,0:T(8,128)(2,1)S(1)}, u32[]{:S(2)}, u32[]{:S(2)}) collective-permute-start(bf16[400,256]{1,0:T(8,128)(2,1)} %get-tuple-element.33), channel_id=1, source_target_pairs={{0,64},{16,80},{32,96},{48,112},{64,0},{80,16},{96,32},{112,48},{1... | collective-permute-start | bytes 614408 | tf_op jit(solution)/shard_map/ppermute | solution.py:383
  9.5 2.9 %collective-permute-start.1 = (bf16[400,256]{1,0:T(8,128)(2,1)}, bf16[400,256]{1,0:T(8,128)(2,1)S(1)}, u32[]{:S(2)}, u32[]{:S(2)}) collective-permute-start(bf16[400,256]{1,0:T(8,128)(2,1)} %get-tuple-element.34), channel_id=1, source_target_pairs={{0,128},{16,144},{32,160},{48,176},{64,192},{80,208},{96,224},{112... | collective-permute-start | bytes 614408 | tf_op jit(solution)/shard_map/ppermute | solution.py:383
  12.6 7.0 %elementals.3 = (f32[384,256]{1,0:T(8,128)}, bf16[400,256]{1,0:T(8,128)(2,1)}, bf16[400,256]{1,0:T(8,128)(2,1)}, bf16[400,256]{1,0:T(8,128)(2,1)}) custom-call(s32[1]{0:T(128)} %copy.8.source, s32[3,3]{1,0:T(4,128)} %mom.3, s32[2]{0:T(128)} %slices.3, s32[2]{0:T(128)} %moments.3, bf16[2,2,1728,256]{3,2,1,0:T(8,128)(2,1)} %bitcast.19), custom_call_target="tpu_custom_call" | custom-call | tf_op jit(solution)/shard_map/elementals/pallas_call | solution.py:160
  20.1 4.1 %collective-permute-start.7 = (bf16[400,256]{1,0:T(8,128)(2,1)}, bf16[400,256]{1,0:T(8,128)(2,1)S(1)}, u32[]{:S(2)}, u32[]{:S(2)}) collective-permute-start(bf16[400,256]{1,0:T(8,128)(2,1)} %get-tuple-element.43), channel_id=1, source_target_pairs={{0,128},{16,144},{32,160},{48,176},{64,192},{80,208},{96,224},{112... | collective-permute-start | bytes 614408 | tf_op jit(solution)/shard_map/ppermute | solution.py:383
  24.6 2.1 %collective-permute-start.3 = (bf16[96,256]{1,0:T(8,128)(2,1)S(1)}, bf16[96,256]{1,0:T(8,128)(2,1)S(1)}, u32[]{:S(2)}, u32[]{:S(2)}) collective-permute-start(bf16[96,256]{1,0:T(8,128)(2,1)S(1)} %get-tuple-element.38), channel_id=1, source_target_pairs={{0,16},{16,0},{32,48},{48,32},{64,80},{80,64},{96,112},{112,96},{1... | collective-permute-start | bytes 147464 | tf_op jit(solution)/shard_map/ppermute | solution.py:387
  26.6 1.6 %collective-permute-start.4 = (bf16[96,256]{1,0:T(8,128)(2,1)S(1)}, bf16[96,256]{1,0:T(8,128)(2,1)S(1)}, u32[]{:S(2)}, u32[]{:S(2)}) collective-permute-start(bf16[96,256]{1,0:T(8,128)(2,1)S(1)} %get-tuple-element.39), channel_id=1, source_target_pairs={{0,32},{16,48},{32,0},{48,16},{64,96},{80,112},{96,64},{112,80},{1... | collective-permute-start | bytes 147464 | tf_op jit(solution)/shard_map/ppermute | solution.py:387
  28.2 1.6 %collective-permute-start.5 = (bf16[96,256]{1,0:T(8,128)(2,1)S(1)}, bf16[96,256]{1,0:T(8,128)(2,1)S(1)}, u32[]{:S(2)}, u32[]{:S(2)}) collective-permute-start(bf16[96,256]{1,0:T(8,128)(2,1)S(1)} %get-tuple-element.40), channel_id=1, source_target_pairs={{0,48},{16,32},{32,16},{48,0},{64,112},{80,96},{96,80},{112,64},{1... | collective-permute-start | bytes 147464 | tf_op jit(solution)/shard_map/ppermute | solution.py:387
  29.8 3.1 %collective-permute-done.7.got2 = bf16[400,256]{1,0:T(8,128)(2,1)S(1)} collective-permute-done((bf16[400,256]{1,0:T(8,128)(2,1)}, bf16[400,256]{1,0:T(8,128)(2,1)S(1)}, u32[]{:S(2)}, u32[]{:S(2)}) %collective-permute-start.7) | collective-permute-done | bytes 204832 | tf_op jit(solution)/shard_map/ppermute | solution.py:383
  32.8 2.4 %collective-permute-done.8.got3 = bf16[400,256]{1,0:T(8,128)(2,1)S(1)} collective-permute-done((bf16[400,256]{1,0:T(8,128)(2,1)}, bf16[400,256]{1,0:T(8,128)(2,1)S(1)}, u32[]{:S(2)}, u32[]{:S(2)}) %collective-permute-start.8) | collective-permute-done | bytes 204832 | tf_op jit(solution)/shard_map/ppermute | solution.py:383
  36.4 3.4 %collective-permute-start.10 = (bf16[96,256]{1,0:T(8,128)(2,1)S(1)}, bf16[96,256]{1,0:T(8,128)(2,1)S(1)}, u32[]{:S(2)}, u32[]{:S(2)}) collective-permute-start(bf16[96,256]{1,0:T(8,128)(2,1)S(1)} %get-tuple-element.47), channel_id=1, source_target_pairs={{0,32},{16,48},{32,0},{48,16},{64,96},{80,112},{96,64},{112,80},{1... | collective-permute-start | bytes 147464 | tf_op jit(solution)/shard_map/ppermute | solution.py:387
  39.9 2.8 %collective-permute-start.15 = (bf16[3,2,16,256]{3,2,1,0:T(8,128)(2,1)S(1)}, bf16[3,2,16,256]{3,2,1,0:T(8,128)(2,1)S(1)}, u32[]{:S(2)}, u32[]{:S(2)}) collective-permute-start(bf16[3,2,16,256]{3,2,1,0:T(8,128)(2,1)S(1)} %bitcast.20), channel_id=1, source_target_pairs={{0,6},{1,7},{2,4},{3,5},{4,2},{5,3},{6,0},{7,1},{8,14},{9,15},{10,... | collective-permute-start | bytes 147464 | tf_op jit(solution)/shard_map/ppermute | solution.py:408
  44.2 1.6 %collective-permute-done.15 = bf16[3,2,16,256]{3,2,1,0:T(8,128)(2,1)S(1)} collective-permute-done((bf16[3,2,16,256]{3,2,1,0:T(8,128)(2,1)S(1)}, bf16[3,2,16,256]{3,2,1,0:T(8,128)(2,1)S(1)}, u32[]{:S(2)}, u32[]{:S(2)}) %collective-permute-start.15) | collective-permute-done | bytes 49184 | tf_op jit(solution)/shard_map/ppermute | solution.py:408
  45.8 1.6 %collective-permute-start.9 = (bf16[96,256]{1,0:T(8,128)(2,1)S(1)}, bf16[96,256]{1,0:T(8,128)(2,1)S(1)}, u32[]{:S(2)}, u32[]{:S(2)}) collective-permute-start(bf16[96,256]{1,0:T(8,128)(2,1)S(1)} %get-tuple-element.46), channel_id=1, source_target_pairs={{0,16},{16,0},{32,48},{48,32},{64,80},{80,64},{96,112},{112,96},{1... | collective-permute-start | bytes 147464 | tf_op jit(solution)/shard_map/ppermute | solution.py:387
  48.4 5.6 %collective-permute-start.18 = (bf16[3,2,16,256]{3,2,1,0:T(8,128)(2,1)S(1)}, bf16[3,2,16,256]{3,2,1,0:T(8,128)(2,1)S(1)}, u32[]{:S(2)}, u32[]{:S(2)}) collective-permute-start(bf16[3,2,16,256]{3,2,1,0:T(8,128)(2,1)S(1)} %select_select_fusion), channel_id=1, source_target_pairs={{0,40},{1,41},{2,42},{3,43},{4,44},{5,45},{6,46},{7,47},{8,32},{9,... | collective-permute-start | bytes 147464 | tf_op jit(solution)/shard_map/ppermute | solution.py:410
  54.1 2.1 %collective-permute-done.18 = bf16[3,2,16,256]{3,2,1,0:T(8,128)(2,1)S(1)} collective-permute-done((bf16[3,2,16,256]{3,2,1,0:T(8,128)(2,1)S(1)}, bf16[3,2,16,256]{3,2,1,0:T(8,128)(2,1)S(1)}, u32[]{:S(2)}, u32[]{:S(2)}) %collective-permute-start.18) | collective-permute-done | bytes 49184 | tf_op jit(solution)/shard_map/ppermute | solution.py:410
  56.3 1.2 %collective-permute-done.19 = bf16[3,2,16,256]{3,2,1,0:T(8,128)(2,1)S(1)} collective-permute-done((bf16[3,2,16,256]{3,2,1,0:T(8,128)(2,1)S(1)}, bf16[3,2,16,256]{3,2,1,0:T(8,128)(2,1)S(1)}, u32[]{:S(2)}, u32[]{:S(2)}) %collective-permute-start.19) | collective-permute-done | bytes 49184 | tf_op jit(solution)/shard_map/ppermute | solution.py:412
  57.7 2.8 %collective-permute-start.21 = (bf16[3,2,16,256]{3,2,1,0:T(8,128)(2,1)S(1)}, bf16[3,2,16,256]{3,2,1,0:T(8,128)(2,1)S(1)}, u32[]{:S(2)}, u32[]{:S(2)}) collective-permute-start(bf16[3,2,16,256]{3,2,1,0:T(8,128)(2,1)S(1)} %broadcast_select_fusion.1.p0), channel_id=1, source_target_pairs={{0,32},{16,48},{32,0},{48,16},{64,96},{80,112},{96,64},{112,80},{1... | collective-permute-start | bytes 147464 | tf_op jit(solution)/shard_map/ppermute | solution.py:387
  62.1 1.7 %collective-permute-done.21.p2 = bf16[3,2,16,256]{3,2,1,0:T(8,128)(2,1)S(1)} collective-permute-done((bf16[3,2,16,256]{3,2,1,0:T(8,128)(2,1)S(1)}, bf16[3,2,16,256]{3,2,1,0:T(8,128)(2,1)S(1)}, u32[]{:S(2)}, u32[]{:S(2)}) %collective-permute-start.21) | collective-permute-done | bytes 49184 | tf_op jit(solution)/shard_map/ppermute | solution.py:387
  63.8 2.0 %collective-permute-done.22.p3 = bf16[3,2,16,256]{3,2,1,0:T(8,128)(2,1)S(1)} collective-permute-done((bf16[3,2,16,256]{3,2,1,0:T(8,128)(2,1)S(1)}, bf16[3,2,16,256]{3,2,1,0:T(8,128)(2,1)S(1)}, u32[]{:S(2)}, u32[]{:S(2)}) %collective-permute-start.22) | collective-permute-done | bytes 49184 | tf_op jit(solution)/shard_map/ppermute | solution.py:387
  66.5 1.0 %collective-permute-start.12 = (bf16[6,2,16,256]{3,2,1,0:T(8,128)(2,1)S(1)}, bf16[6,2,16,256]{3,2,1,0:T(8,128)(2,1)S(1)}, u32[]{:S(2)}, u32[]{:S(2)}) collective-permute-start(bf16[6,2,16,256]{3,2,1,0:T(8,128)(2,1)S(1)} %pad_maximum_fusion.p0), channel_id=1, source_target_pairs={{0,16},{16,0},{32,48},{48,32},{64,80},{80,64},{96,112},{112,96},{1... | collective-permute-start | bytes 294920 | tf_op jit(solution)/shard_map/ppermute | solution.py:387
  67.5 1.8 %collective-permute-start.13 = (bf16[6,2,16,256]{3,2,1,0:T(8,128)(2,1)S(1)}, bf16[6,2,16,256]{3,2,1,0:T(8,128)(2,1)S(1)}, u32[]{:S(2)}, u32[]{:S(2)}) collective-permute-start(bf16[6,2,16,256]{3,2,1,0:T(8,128)(2,1)S(1)} %pad_maximum_fusion.p0), channel_id=1, source_target_pairs={{0,32},{16,48},{32,0},{48,16},{64,96},{80,112},{96,64},{112,80},{1... | collective-permute-start | bytes 294920 | tf_op jit(solution)/shard_map/ppermute | solution.py:387
  70.1 1.8 %collective-permute-start.27 = (bf16[2,4,2,16,256]{4,3,2,1,0:T(8,128)(2,1)S(1)}, bf16[2,4,2,16,256]{4,3,2,1,0:T(8,128)(2,1)S(1)}, u32[]{:S(2)}, u32[]{:S(2)}) collective-permute-start(bf16[2,4,2,16,256]{4,3,2,1,0:T(8,128)(2,1)S(1)} %get-tuple-element.51), channel_id=1, source_target_pairs={{0,128},{16,144},{32,160},{48,176},{64,192},{80,208},{96,224},{112... | collective-permute-start | bytes 393224 | tf_op jit(solution)/shard_map/ppermute | solution.py:383
  72.3 2.5 %collective-permute-start.28 = (bf16[2,4,2,16,256]{4,3,2,1,0:T(8,128)(2,1)S(1)}, bf16[2,4,2,16,256]{4,3,2,1,0:T(8,128)(2,1)S(1)}, u32[]{:S(2)}, u32[]{:S(2)}) collective-permute-start(bf16[2,4,2,16,256]{4,3,2,1,0:T(8,128)(2,1)S(1)} %get-tuple-element.52), channel_id=1, source_target_pairs={{0,192},{16,208},{32,224},{48,240},{64,128},{80,144},{96,160},{112... | collective-permute-start | bytes 393224 | tf_op jit(solution)/shard_map/ppermute | solution.py:383
  74.8 1.0 %collective-permute-done.13.p2 = bf16[6,2,16,256]{3,2,1,0:T(8,128)(2,1)S(1)} collective-permute-done((bf16[6,2,16,256]{3,2,1,0:T(8,128)(2,1)S(1)}, bf16[6,2,16,256]{3,2,1,0:T(8,128)(2,1)S(1)}, u32[]{:S(2)}, u32[]{:S(2)}) %collective-permute-start.13) | collective-permute-done | bytes 98336 | tf_op jit(solution)/shard_map/ppermute | solution.py:387
  75.8 2.6 %collective-permute-done.14.p3 = bf16[6,2,16,256]{3,2,1,0:T(8,128)(2,1)S(1)} collective-permute-done((bf16[6,2,16,256]{3,2,1,0:T(8,128)(2,1)S(1)}, bf16[6,2,16,256]{3,2,1,0:T(8,128)(2,1)S(1)}, u32[]{:S(2)}, u32[]{:S(2)}) %collective-permute-start.14) | collective-permute-done | bytes 98336 | tf_op jit(solution)/shard_map/ppermute | solution.py:387
  79.0 1.8 %collective-permute-start.23 = (bf16[2,4,2,16,256]{4,3,2,1,0:T(8,128)(2,1)S(1)}, bf16[2,4,2,16,256]{4,3,2,1,0:T(8,128)(2,1)S(1)}, u32[]{:S(2)}, u32[]{:S(2)}) collective-permute-start(bf16[2,4,2,16,256]{4,3,2,1,0:T(8,128)(2,1)S(1)} %get-tuple-element.58), channel_id=1, source_target_pairs={{0,64},{16,80},{32,96},{48,112},{64,0},{80,16},{96,32},{112,48},{1... | collective-permute-start | bytes 393224 | tf_op jit(solution)/shard_map/ppermute | solution.py:383
  80.9 2.9 %collective-permute-start.25 = (bf16[2,4,2,16,256]{4,3,2,1,0:T(8,128)(2,1)S(1)}, bf16[2,4,2,16,256]{4,3,2,1,0:T(8,128)(2,1)S(1)}, u32[]{:S(2)}, u32[]{:S(2)}) collective-permute-start(bf16[2,4,2,16,256]{4,3,2,1,0:T(8,128)(2,1)S(1)} %get-tuple-element.60), channel_id=1, source_target_pairs={{0,192},{16,208},{32,224},{48,240},{64,128},{80,144},{96,160},{112... | collective-permute-start | bytes 393224 | tf_op jit(solution)/shard_map/ppermute | solution.py:383
  83.8 2.2 %copy-done = bf16[2,2,1024,512]{3,2,1,0:T(8,128)(2,1)S(1)} copy-done((bf16[2,2,1024,512]{3,2,1,0:T(8,128)(2,1)S(1)}, bf16[2,2,1024,512]{3,2,1,0:T(8,128)(2,1)}, u32[]{:S(2)}) %copy-start) | copy-done | bytes 4194328
  86.0 2.2 %transpose_tau.1.tt_ref = bf16[2,512,2048]{2,1,0:T(8,128)(2,1)S(1)} custom-call(bf16[2,2,4,256,512]{4,3,2,1,0:T(8,128)(2,1)S(1)} %bitcast.16), custom_call_target="tpu_custom_call" | custom-call | tf_op jit(solution)/shard_map/transpose_tau/pallas_call | solution.py:213
  88.3 7.0 %middle.1.m_ref = bf16[2,512,1024]{2,1,0:T(8,128)(2,1)S(1)} custom-call(s32[1]{0:T(128)} %copy.8.source, bf16[2,4,2,16,256]{4,3,2,1,0:T(8,128)(2,1)S(1)} %get-tuple-element.49.f0, bf16[2,4,2,16,256]{4,3,2,1,0:T(8,128)(2,1)S(1)} %collective-permute-done.26.f1, bf16[2,4,2,16,256]{4,3,2,1,0:T(8,128)(2,1)S(1)} %collective-permute-done.27.f2, ...), custom_call_target="tpu_custom_call" | custom-call | tf_op jit(solution)/shard_map/middle/pallas_call | solution.py:286
  95.3 3.3 %outer.1 = bf16[2,2,512,512]{3,2,1,0:T(8,128)(2,1)} custom-call(s32[4]{0:T(128)S(1)} %copy-done.4, bf16[2,4,2,16,256]{4,3,2,1,0:T(8,128)(2,1)S(1)} %get-tuple-element.57.s0, bf16[2,4,2,16,256]{4,3,2,1,0:T(8,128)(2,1)S(1)} %collective-permute-done.23.s1, bf16[2,4,2,16,256]{4,3,2,1,0:T(8,128)(2,1)S(1)} %collective-permute-done.24.s2, ...), custom_call_target="tpu_custom_call" | custom-call | tf_op jit(solution)/shard_map/outer/pallas_call | solution.py:350
  (60 shorter events, 9.4 us)
Async XLA Ops:
  0.7 23.8 %copy-start.5 = (s32[2]{0:T(128)S(1)}, s32[2]{0:T(128)}, u32[]{:S(2)}) copy-start(s32[2]{0:T(128)} %slices.3) | copy-start | bytes 28
  0.7 23.8 %copy-start.6 = (s32[2]{0:T(128)S(1)}, s32[2]{0:T(128)}, u32[]{:S(2)}) copy-start(s32[2]{0:T(128)} %moments.3) | copy-start | bytes 28
  7.8 16.6 %copy-start.3 = (f32[384,256]{1,0:T(8,128)S(1)}, f32[384,256]{1,0:T(8,128)}, u32[]{:S(2)}) copy-start(f32[384,256]{1,0:T(8,128)} %get-tuple-element.36.kept) | copy-start | bytes 1179652
  7.8 16.4 %collective-permute-start = (bf16[400,256]{1,0:T(8,128)(2,1)}, bf16[400,256]{1,0:T(8,128)(2,1)S(1)}, u32[]{:S(2)}, u32[]{:S(2)}) collective-permute-start(bf16[400,256]{1,0:T(8,128)(2,1)} %get-tuple-element.33), channel_id=1, source_target_pairs={{0,64},{16,80},{32,96},{48,112},{64,0},{80,16},{96,32},{112,48},{1... | collective-permute-start | bytes 614408 | tf_op jit(solution)/shard_map/ppermute | solution.py:383
  9.5 14.9 %collective-permute-start.1 = (bf16[400,256]{1,0:T(8,128)(2,1)}, bf16[400,256]{1,0:T(8,128)(2,1)S(1)}, u32[]{:S(2)}, u32[]{:S(2)}) collective-permute-start(bf16[400,256]{1,0:T(8,128)(2,1)} %get-tuple-element.34), channel_id=1, source_target_pairs={{0,128},{16,144},{32,160},{48,176},{64,192},{80,208},{96,224},{112... | collective-permute-start | bytes 614408 | tf_op jit(solution)/shard_map/ppermute | solution.py:383
  12.4 12.1 %collective-permute-start.2 = (bf16[400,256]{1,0:T(8,128)(2,1)}, bf16[400,256]{1,0:T(8,128)(2,1)S(1)}, u32[]{:S(2)}, u32[]{:S(2)}) collective-permute-start(bf16[400,256]{1,0:T(8,128)(2,1)} %get-tuple-element.35), channel_id=1, source_target_pairs={{0,192},{16,208},{32,224},{48,240},{64,128},{80,144},{96,160},{112... | collective-permute-start | bytes 614408 | tf_op jit(solution)/shard_map/ppermute | solution.py:383
  19.6 8.6 %collective-permute-start.6 = (bf16[400,256]{1,0:T(8,128)(2,1)}, bf16[400,256]{1,0:T(8,128)(2,1)S(1)}, u32[]{:S(2)}, u32[]{:S(2)}) collective-permute-start(bf16[400,256]{1,0:T(8,128)(2,1)} %get-tuple-element.42), channel_id=1, source_target_pairs={{0,64},{16,80},{32,96},{48,112},{64,0},{80,16},{96,32},{112,48},{1... | collective-permute-start | bytes 614408 | tf_op jit(solution)/shard_map/ppermute | solution.py:383
  20.1 12.8 %collective-permute-start.7 = (bf16[400,256]{1,0:T(8,128)(2,1)}, bf16[400,256]{1,0:T(8,128)(2,1)S(1)}, u32[]{:S(2)}, u32[]{:S(2)}) collective-permute-start(bf16[400,256]{1,0:T(8,128)(2,1)} %get-tuple-element.43), channel_id=1, source_target_pairs={{0,128},{16,144},{32,160},{48,176},{64,192},{80,208},{96,224},{112... | collective-permute-start | bytes 614408 | tf_op jit(solution)/shard_map/ppermute | solution.py:383
  24.2 11.1 %collective-permute-start.8 = (bf16[400,256]{1,0:T(8,128)(2,1)}, bf16[400,256]{1,0:T(8,128)(2,1)S(1)}, u32[]{:S(2)}, u32[]{:S(2)}) collective-permute-start(bf16[400,256]{1,0:T(8,128)(2,1)} %get-tuple-element.44), channel_id=1, source_target_pairs={{0,192},{16,208},{32,224},{48,240},{64,128},{80,144},{96,160},{112... | collective-permute-start | bytes 614408 | tf_op jit(solution)/shard_map/ppermute | solution.py:383
  24.6 15.3 %collective-permute-start.3 = (bf16[96,256]{1,0:T(8,128)(2,1)S(1)}, bf16[96,256]{1,0:T(8,128)(2,1)S(1)}, u32[]{:S(2)}, u32[]{:S(2)}) collective-permute-start(bf16[96,256]{1,0:T(8,128)(2,1)S(1)} %get-tuple-element.38), channel_id=1, source_target_pairs={{0,16},{16,0},{32,48},{48,32},{64,80},{80,64},{96,112},{112,96},{1... | collective-permute-start | bytes 147464 | tf_op jit(solution)/shard_map/ppermute | solution.py:387
  26.6 13.2 %collective-permute-start.4 = (bf16[96,256]{1,0:T(8,128)(2,1)S(1)}, bf16[96,256]{1,0:T(8,128)(2,1)S(1)}, u32[]{:S(2)}, u32[]{:S(2)}) collective-permute-start(bf16[96,256]{1,0:T(8,128)(2,1)S(1)} %get-tuple-element.39), channel_id=1, source_target_pairs={{0,32},{16,48},{32,0},{48,16},{64,96},{80,112},{96,64},{112,80},{1... | collective-permute-start | bytes 147464 | tf_op jit(solution)/shard_map/ppermute | solution.py:387
  28.2 11.7 %collective-permute-start.5 = (bf16[96,256]{1,0:T(8,128)(2,1)S(1)}, bf16[96,256]{1,0:T(8,128)(2,1)S(1)}, u32[]{:S(2)}, u32[]{:S(2)}) collective-permute-start(bf16[96,256]{1,0:T(8,128)(2,1)S(1)} %get-tuple-element.40), channel_id=1, source_target_pairs={{0,48},{16,32},{32,16},{48,0},{64,112},{80,96},{96,80},{112,64},{1... | collective-permute-start | bytes 147464 | tf_op jit(solution)/shard_map/ppermute | solution.py:387
  36.4 24.1 %collective-permute-start.10 = (bf16[96,256]{1,0:T(8,128)(2,1)S(1)}, bf16[96,256]{1,0:T(8,128)(2,1)S(1)}, u32[]{:S(2)}, u32[]{:S(2)}) collective-permute-start(bf16[96,256]{1,0:T(8,128)(2,1)S(1)} %get-tuple-element.47), channel_id=1, source_target_pairs={{0,32},{16,48},{32,0},{48,16},{64,96},{80,112},{96,64},{112,80},{1... | collective-permute-start | bytes 147464 | tf_op jit(solution)/shard_map/ppermute | solution.py:387
  39.7 21.4 %collective-permute-start.11 = (bf16[96,256]{1,0:T(8,128)(2,1)S(1)}, bf16[96,256]{1,0:T(8,128)(2,1)S(1)}, u32[]{:S(2)}, u32[]{:S(2)}) collective-permute-start(bf16[96,256]{1,0:T(8,128)(2,1)S(1)} %get-tuple-element.48), channel_id=1, source_target_pairs={{0,48},{16,32},{32,16},{48,0},{64,112},{80,96},{96,80},{112,64},{1... | collective-permute-start | bytes 147464 | tf_op jit(solution)/shard_map/ppermute | solution.py:387
  39.9 5.9 %collective-permute-start.15 = (bf16[3,2,16,256]{3,2,1,0:T(8,128)(2,1)S(1)}, bf16[3,2,16,256]{3,2,1,0:T(8,128)(2,1)S(1)}, u32[]{:S(2)}, u32[]{:S(2)}) collective-permute-start(bf16[3,2,16,256]{3,2,1,0:T(8,128)(2,1)S(1)} %bitcast.20), channel_id=1, source_target_pairs={{0,6},{1,7},{2,4},{3,5},{4,2},{5,3},{6,0},{7,1},{8,14},{9,15},{10,... | collective-permute-start | bytes 147464 | tf_op jit(solution)/shard_map/ppermute | solution.py:408
  42.8 5.6 %collective-permute-start.16 = (bf16[3,2,16,256]{3,2,1,0:T(8,128)(2,1)S(1)}, bf16[3,2,16,256]{3,2,1,0:T(8,128)(2,1)S(1)}, u32[]{:S(2)}, u32[]{:S(2)}) collective-permute-start(bf16[3,2,16,256]{3,2,1,0:T(8,128)(2,1)S(1)} %bitcast.21), channel_id=1, source_target_pairs={{0,4},{1,5},{2,6},{3,7},{4,0},{5,1},{6,2},{7,3},{8,12},{9,13},{10,... | collective-permute-start | bytes 147464 | tf_op jit(solution)/shard_map/ppermute | solution.py:408
  43.6 4.8 %collective-permute-start.17 = (bf16[3,2,16,256]{3,2,1,0:T(8,128)(2,1)S(1)}, bf16[3,2,16,256]{3,2,1,0:T(8,128)(2,1)S(1)}, u32[]{:S(2)}, u32[]{:S(2)}) collective-permute-start(bf16[3,2,16,256]{3,2,1,0:T(8,128)(2,1)S(1)} %bitcast.22), channel_id=1, source_target_pairs={{0,2},{1,3},{2,0},{3,1},{4,6},{5,7},{6,4},{7,5},{8,10},{9,11},{10,... | collective-permute-start | bytes 147464 | tf_op jit(solution)/shard_map/ppermute | solution.py:408
  45.8 15.3 %collective-permute-start.9 = (bf16[96,256]{1,0:T(8,128)(2,1)S(1)}, bf16[96,256]{1,0:T(8,128)(2,1)S(1)}, u32[]{:S(2)}, u32[]{:S(2)}) collective-permute-start(bf16[96,256]{1,0:T(8,128)(2,1)S(1)} %get-tuple-element.46), channel_id=1, source_target_pairs={{0,16},{16,0},{32,48},{48,32},{64,80},{80,64},{96,112},{112,96},{1... | collective-permute-start | bytes 147464 | tf_op jit(solution)/shard_map/ppermute | solution.py:387
  48.4 7.8 %collective-permute-start.18 = (bf16[3,2,16,256]{3,2,1,0:T(8,128)(2,1)S(1)}, bf16[3,2,16,256]{3,2,1,0:T(8,128)(2,1)S(1)}, u32[]{:S(2)}, u32[]{:S(2)}) collective-permute-start(bf16[3,2,16,256]{3,2,1,0:T(8,128)(2,1)S(1)} %select_select_fusion), channel_id=1, source_target_pairs={{0,40},{1,41},{2,42},{3,43},{4,44},{5,45},{6,46},{7,47},{8,32},{9,... | collective-permute-start | bytes 147464 | tf_op jit(solution)/shard_map/ppermute | solution.py:410
  56.2 1.3 %collective-permute-start.19 = (bf16[3,2,16,256]{3,2,1,0:T(8,128)(2,1)S(1)}, bf16[3,2,16,256]{3,2,1,0:T(8,128)(2,1)S(1)}, u32[]{:S(2)}, u32[]{:S(2)}) collective-permute-start(bf16[3,2,16,256]{3,2,1,0:T(8,128)(2,1)S(1)} %broadcast_select_fusion), channel_id=1, source_target_pairs={{0,1},{1,0},{2,3},{3,2},{4,5},{5,4},{6,7},{7,6},{8,9},{9,8},{10,11... | collective-permute-start | bytes 147464 | tf_op jit(solution)/shard_map/ppermute | solution.py:412
  57.5 4.6 %collective-permute-start.20 = (bf16[3,2,16,256]{3,2,1,0:T(8,128)(2,1)S(1)}, bf16[3,2,16,256]{3,2,1,0:T(8,128)(2,1)S(1)}, u32[]{:S(2)}, u32[]{:S(2)}) collective-permute-start(bf16[3,2,16,256]{3,2,1,0:T(8,128)(2,1)S(1)} %broadcast_select_fusion.1.p0), channel_id=1, source_target_pairs={{0,16},{16,0},{32,48},{48,32},{64,80},{80,64},{96,112},{112,96},{1... | collective-permute-start | bytes 147464 | tf_op jit(solution)/shard_map/ppermute | solution.py:387
  57.7 6.1 %collective-permute-start.21 = (bf16[3,2,16,256]{3,2,1,0:T(8,128)(2,1)S(1)}, bf16[3,2,16,256]{3,2,1,0:T(8,128)(2,1)S(1)}, u32[]{:S(2)}, u32[]{:S(2)}) collective-permute-start(bf16[3,2,16,256]{3,2,1,0:T(8,128)(2,1)S(1)} %broadcast_select_fusion.1.p0), channel_id=1, source_target_pairs={{0,32},{16,48},{32,0},{48,16},{64,96},{80,112},{96,64},{112,80},{1... | collective-permute-start | bytes 147464 | tf_op jit(solution)/shard_map/ppermute | solution.py:387
  60.5 5.3 %collective-permute-start.22 = (bf16[3,2,16,256]{3,2,1,0:T(8,128)(2,1)S(1)}, bf16[3,2,16,256]{3,2,1,0:T(8,128)(2,1)S(1)}, u32[]{:S(2)}, u32[]{:S(2)}) collective-permute-start(bf16[3,2,16,256]{3,2,1,0:T(8,128)(2,1)S(1)} %broadcast_select_fusion.1.p0), channel_id=1, source_target_pairs={{0,48},{16,32},{32,16},{48,0},{64,112},{80,96},{96,80},{112,64},{1... | collective-permute-start | bytes 147464 | tf_op jit(solution)/shard_map/ppermute | solution.py:387
  66.4 14.5 %collective-permute-start.26 = (bf16[2,4,2,16,256]{4,3,2,1,0:T(8,128)(2,1)S(1)}, bf16[2,4,2,16,256]{4,3,2,1,0:T(8,128)(2,1)S(1)}, u32[]{:S(2)}, u32[]{:S(2)}) collective-permute-start(bf16[2,4,2,16,256]{4,3,2,1,0:T(8,128)(2,1)S(1)} %get-tuple-element.50), channel_id=1, source_target_pairs={{0,64},{16,80},{32,96},{48,112},{64,0},{80,16},{96,32},{112,48},{1... | collective-permute-start | bytes 393224 | tf_op jit(solution)/shard_map/ppermute | solution.py:383
  66.5 5.8 %collective-permute-start.12 = (bf16[6,2,16,256]{3,2,1,0:T(8,128)(2,1)S(1)}, bf16[6,2,16,256]{3,2,1,0:T(8,128)(2,1)S(1)}, u32[]{:S(2)}, u32[]{:S(2)}) collective-permute-start(bf16[6,2,16,256]{3,2,1,0:T(8,128)(2,1)S(1)} %pad_maximum_fusion.p0), channel_id=1, source_target_pairs={{0,16},{16,0},{32,48},{48,32},{64,80},{80,64},{96,112},{112,96},{1... | collective-permute-start | bytes 294920 | tf_op jit(solution)/shard_map/ppermute | solution.py:387
  67.5 8.2 %collective-permute-start.13 = (bf16[6,2,16,256]{3,2,1,0:T(8,128)(2,1)S(1)}, bf16[6,2,16,256]{3,2,1,0:T(8,128)(2,1)S(1)}, u32[]{:S(2)}, u32[]{:S(2)}) collective-permute-start(bf16[6,2,16,256]{3,2,1,0:T(8,128)(2,1)S(1)} %pad_maximum_fusion.p0), channel_id=1, source_target_pairs={{0,32},{16,48},{32,0},{48,16},{64,96},{80,112},{96,64},{112,80},{1... | collective-permute-start | bytes 294920 | tf_op jit(solution)/shard_map/ppermute | solution.py:387
  69.3 9.1 %collective-permute-start.14 = (bf16[6,2,16,256]{3,2,1,0:T(8,128)(2,1)S(1)}, bf16[6,2,16,256]{3,2,1,0:T(8,128)(2,1)S(1)}, u32[]{:S(2)}, u32[]{:S(2)}) collective-permute-start(bf16[6,2,16,256]{3,2,1,0:T(8,128)(2,1)S(1)} %pad_maximum_fusion.p0), channel_id=1, source_target_pairs={{0,48},{16,32},{32,16},{48,0},{64,112},{80,96},{96,80},{112,64},{1... | collective-permute-start | bytes 294920 | tf_op jit(solution)/shard_map/ppermute | solution.py:387
  70.1 18.1 %collective-permute-start.27 = (bf16[2,4,2,16,256]{4,3,2,1,0:T(8,128)(2,1)S(1)}, bf16[2,4,2,16,256]{4,3,2,1,0:T(8,128)(2,1)S(1)}, u32[]{:S(2)}, u32[]{:S(2)}) collective-permute-start(bf16[2,4,2,16,256]{4,3,2,1,0:T(8,128)(2,1)S(1)} %get-tuple-element.51), channel_id=1, source_target_pairs={{0,128},{16,144},{32,160},{48,176},{64,192},{80,208},{96,224},{112... | collective-permute-start | bytes 393224 | tf_op jit(solution)/shard_map/ppermute | solution.py:383
  72.3 16.0 %collective-permute-start.28 = (bf16[2,4,2,16,256]{4,3,2,1,0:T(8,128)(2,1)S(1)}, bf16[2,4,2,16,256]{4,3,2,1,0:T(8,128)(2,1)S(1)}, u32[]{:S(2)}, u32[]{:S(2)}) collective-permute-start(bf16[2,4,2,16,256]{4,3,2,1,0:T(8,128)(2,1)S(1)} %get-tuple-element.52), channel_id=1, source_target_pairs={{0,192},{16,208},{32,224},{48,240},{64,128},{80,144},{96,160},{112... | collective-permute-start | bytes 393224 | tf_op jit(solution)/shard_map/ppermute | solution.py:383
  79.0 16.2 %collective-permute-start.23 = (bf16[2,4,2,16,256]{4,3,2,1,0:T(8,128)(2,1)S(1)}, bf16[2,4,2,16,256]{4,3,2,1,0:T(8,128)(2,1)S(1)}, u32[]{:S(2)}, u32[]{:S(2)}) collective-permute-start(bf16[2,4,2,16,256]{4,3,2,1,0:T(8,128)(2,1)S(1)} %get-tuple-element.58), channel_id=1, source_target_pairs={{0,64},{16,80},{32,96},{48,112},{64,0},{80,16},{96,32},{112,48},{1... | collective-permute-start | bytes 393224 | tf_op jit(solution)/shard_map/ppermute | solution.py:383
  80.8 14.4 %collective-permute-start.24 = (bf16[2,4,2,16,256]{4,3,2,1,0:T(8,128)(2,1)S(1)}, bf16[2,4,2,16,256]{4,3,2,1,0:T(8,128)(2,1)S(1)}, u32[]{:S(2)}, u32[]{:S(2)}) collective-permute-start(bf16[2,4,2,16,256]{4,3,2,1,0:T(8,128)(2,1)S(1)} %get-tuple-element.59), channel_id=1, source_target_pairs={{0,128},{16,144},{32,160},{48,176},{64,192},{80,208},{96,224},{112... | collective-permute-start | bytes 393224 | tf_op jit(solution)/shard_map/ppermute | solution.py:383
  80.9 14.3 %collective-permute-start.25 = (bf16[2,4,2,16,256]{4,3,2,1,0:T(8,128)(2,1)S(1)}, bf16[2,4,2,16,256]{4,3,2,1,0:T(8,128)(2,1)S(1)}, u32[]{:S(2)}, u32[]{:S(2)}) collective-permute-start(bf16[2,4,2,16,256]{4,3,2,1,0:T(8,128)(2,1)S(1)} %get-tuple-element.60), channel_id=1, source_target_pairs={{0,192},{16,208},{32,224},{48,240},{64,128},{80,144},{96,160},{112... | collective-permute-start | bytes 393224 | tf_op jit(solution)/shard_map/ppermute | solution.py:383
  (4 other events, 12.5 us)
where the time goes:
time: 98.9 us; the launch traced here: 98.6 us
  starting transfers between devices  45.9 us (46%)
  Pallas kernels  28 us (28%)
  waiting for transfers between devices  20.2 us (20%)
  local copies, waits for them, and re-layouts  3.21 us (3%)
    ppermute x12, starting transfers between devices, swap_y(): got[step] = lax.ppermute(parts[step], 'site', y_swap(step))  18.7 us
    ppermute x12, starting transfers between devices, swap_z(): lax.ppermute(parts[step], 'site', z_swap(step))  17.3 us
    pallas_call x2, Pallas kernels, partial_elementals(): pl.pallas_call(functools.partial(elementals_kernel, turned), in_specs=[sm...  14.1 us
    ppermute x12, waiting for transfers between devices, swap_z(): lax.ppermute(parts[step], 'site', z_swap(step))  8.71 us
    pallas_call x1, Pallas kernels, middle_of(): pl.pallas_call(middle_kernel, grid_spec=pltpu.PrefetchScalarGridSpec(num_...  6.96 us
    ppermute x1, starting transfers between devices, body(): got = lax.ppermute(held, ('site', 'cuts'), half_swap())  5.58 us
    ppermute x12, waiting for transfers between devices, swap_y(): got[step] = lax.ppermute(parts[step], 'site', y_swap(step))  5.55 us
    ppermute x3, starting transfers between devices, body(): got = lax.ppermute(chunk_a, 'cuts', cut_swap(step, 0))  4.18 us
  transfers between devices with their start and end apart: 29, of which 12 were waited for; matrix products, arithmetic and copies ran while one was open for 0% of the time, Pallas kernels for 17%

commit v1 on v0

--- a/solution.py
+++ b/solution.py
@@ -102,7 +102,7 @@
     columns = trig[...].T
     for q in range(2 * NMOM):
         wide_trig[q] = jnp.broadcast_to(columns[:count, q : q + 1], (count, 128))
-    phased[depth:, :] = jnp.zeros((padded - depth, 2 * NVEC), BF16)
+    phased[:, depth:, :] = jnp.zeros((NMOM, padded - depth, 2 * NVEC), BF16)
     waited = 0
     for first in range(0, padded, 128):
         rows = min(128, depth - first)
@@ -123,11 +123,11 @@
                 imag = vbuf[1, rows, cols].astype(F32)
                 cosine = wide_trig[p]
                 sine = wide_trig[p + NMOM]
-                phased[rows, half * 128 : half * 128 + 128] = (cosine * real + sine * imag).astype(BF16)
-                phased[rows, NVEC + half * 128 : NVEC + half * 128 + 128] = (
+                phased[p, rows, half * 128 : half * 128 + 128] = (cosine * real + sine * imag).astype(BF16)
+                phased[p, rows, NVEC + half * 128 : NVEC + half * 128 + 128] = (
                     cosine * imag - sine * real
                 ).astype(BF16)
-        product = jnp.dot(flipped[...], phased[...], preferred_element_type=F32)
+        product = jnp.dot(flipped[...], phased[p], preferred_element_type=F32)
         acc[2 * p] = product[:NVEC, :NVEC] + product[NVEC:, NVEC:]
         acc[2 * p + 1] = product[:NVEC, NVEC:] - product[NVEC:, :NVEC]
     rows = NVEC // YN
@@ -166,7 +166,7 @@
             pltpu.VMEM((8, -(-count // 128) * 128), F32),
             pltpu.VMEM((2 * NMOM, count, 128), F32),
             pltpu.VMEM((2 * NVEC, padded), BF16),
-            pltpu.VMEM((padded, 2 * NVEC), BF16),
+            pltpu.VMEM((NMOM, padded, 2 * NVEC), BF16),
             pltpu.VMEM((2, depth, NVEC), BF16),
             pltpu.VMEM((height, NVEC), F32),
             pltpu.VMEM((3, height + 16, NVEC), BF16),

time: 98.9 us -> 98.3 us (level)
  transfers between devices with their start and end apart: 29 -> 29, of which waited for: 12 -> 13; matrix products, arithmetic and copies ran while one was open for 0% -> 0% of each run, Pallas kernels for 17% -> 17%
where the time goes in v1:
time: 98.3 us; the launch traced here: 98.1 us
  starting transfers between devices  45.6 us (46%)
  Pallas kernels  27.4 us (28%)
  waiting for transfers between devices  20.4 us (21%)
  local copies, waits for them, and re-layouts  3.21 us (3%)
    ppermute x12, starting transfers between devices, swap_y(): got[step] = lax.ppermute(parts[step], 'site', y_swap(step))  18.7 us
    ppermute x12, starting transfers between devices, swap_z(): lax.ppermute(parts[step], 'site', z_swap(step))  17 us
    pallas_call x2, Pallas kernels, partial_elementals(): pl.pallas_call(functools.partial(elementals_kernel, turned), in_specs=[sm...  13.6 us
    ppermute x12, waiting for transfers between devices, swap_z(): lax.ppermute(parts[step], 'site', z_swap(step))  8.72 us
    pallas_call x1, Pallas kernels, middle_of(): pl.pallas_call(middle_kernel, grid_spec=pltpu.PrefetchScalarGridSpec(num_...  6.96 us
    ppermute x12, waiting for transfers between devices, swap_y(): got[step] = lax.ppermute(parts[step], 'site', y_swap(step))  5.8 us
    ppermute x1, starting transfers between devices, body(): got = lax.ppermute(held, ('site', 'cuts'), half_swap())  5.58 us
    ppermute x3, starting transfers between devices, body(): got = lax.ppermute(chunk_a, 'cuts', cut_swap(step, 0))  4.18 us
  transfers between devices with their start and end apart: 29, of which 13 were waited for; matrix products, arithmetic and copies ran while one was open for 0% of the time, Pallas kernels for 17%

profile of v1, /device:TPU:32, one launch (start us, length us, event | category | flops | bytes accessed | tf_op | source)
XLA Modules:
  0.0 98.1 jit_solution(5200229544198340940)
XLA Ops:
  0.7 6.9 %elementals.2 = (f32[384,256]{1,0:T(8,128)}, bf16[400,256]{1,0:T(8,128)(2,1)}, bf16[400,256]{1,0:T(8,128)(2,1)}, bf16[400,256]{1,0:T(8,128)(2,1)}) custom-call(s32[1]{0:T(128)} %copy.8.source, s32[3,3]{1,0:T(4,128)} %mom.3, s32[2]{0:T(128)} %slices.3, s32[2]{0:T(128)} %moments.3, bf16[2,2,1728,256]{3,2,1,0:T(8,128)(2,1)} %bitcast.18), custom_call_target="tpu_custom_call" | custom-call | tf_op jit(solution)/shard_map/elementals/pallas_call | solution.py:160
  7.6 1.7 %collective-permute-start = (bf16[400,256]{1,0:T(8,128)(2,1)}, bf16[400,256]{1,0:T(8,128)(2,1)S(1)}, u32[]{:S(2)}, u32[]{:S(2)}) collective-permute-start(bf16[400,256]{1,0:T(8,128)(2,1)} %get-tuple-element.33), channel_id=1, source_target_pairs={{0,64},{16,80},{32,96},{48,112},{64,0},{80,16},{96,32},{112,48},{1... | collective-permute-start | bytes 614408 | tf_op jit(solution)/shard_map/ppermute | solution.py:383
  9.2 2.9 %collective-permute-start.1 = (bf16[400,256]{1,0:T(8,128)(2,1)}, bf16[400,256]{1,0:T(8,128)(2,1)S(1)}, u32[]{:S(2)}, u32[]{:S(2)}) collective-permute-start(bf16[400,256]{1,0:T(8,128)(2,1)} %get-tuple-element.34), channel_id=1, source_target_pairs={{0,128},{16,144},{32,160},{48,176},{64,192},{80,208},{96,224},{112... | collective-permute-start | bytes 614408 | tf_op jit(solution)/shard_map/ppermute | solution.py:383
  12.4 6.7 %elementals.3 = (f32[384,256]{1,0:T(8,128)}, bf16[400,256]{1,0:T(8,128)(2,1)}, bf16[400,256]{1,0:T(8,128)(2,1)}, bf16[400,256]{1,0:T(8,128)(2,1)}) custom-call(s32[1]{0:T(128)} %copy.8.source, s32[3,3]{1,0:T(4,128)} %mom.3, s32[2]{0:T(128)} %slices.3, s32[2]{0:T(128)} %moments.3, bf16[2,2,1728,256]{3,2,1,0:T(8,128)(2,1)} %bitcast.19), custom_call_target="tpu_custom_call" | custom-call | tf_op jit(solution)/shard_map/elementals/pallas_call | solution.py:160
  19.6 4.1 %collective-permute-start.7 = (bf16[400,256]{1,0:T(8,128)(2,1)}, bf16[400,256]{1,0:T(8,128)(2,1)S(1)}, u32[]{:S(2)}, u32[]{:S(2)}) collective-permute-start(bf16[400,256]{1,0:T(8,128)(2,1)} %get-tuple-element.43), channel_id=1, source_target_pairs={{0,128},{16,144},{32,160},{48,176},{64,192},{80,208},{96,224},{112... | collective-permute-start | bytes 614408 | tf_op jit(solution)/shard_map/ppermute | solution.py:383
  24.3 1.8 %collective-permute-start.3 = (bf16[96,256]{1,0:T(8,128)(2,1)S(1)}, bf16[96,256]{1,0:T(8,128)(2,1)S(1)}, u32[]{:S(2)}, u32[]{:S(2)}) collective-permute-start(bf16[96,256]{1,0:T(8,128)(2,1)S(1)} %get-tuple-element.38), channel_id=1, source_target_pairs={{0,16},{16,0},{32,48},{48,32},{64,80},{80,64},{96,112},{112,96},{1... | collective-permute-start | bytes 147464 | tf_op jit(solution)/shard_map/ppermute | solution.py:387
  26.1 1.8 %collective-permute-start.4 = (bf16[96,256]{1,0:T(8,128)(2,1)S(1)}, bf16[96,256]{1,0:T(8,128)(2,1)S(1)}, u32[]{:S(2)}, u32[]{:S(2)}) collective-permute-start(bf16[96,256]{1,0:T(8,128)(2,1)S(1)} %get-tuple-element.39), channel_id=1, source_target_pairs={{0,32},{16,48},{32,0},{48,16},{64,96},{80,112},{96,64},{112,80},{1... | collective-permute-start | bytes 147464 | tf_op jit(solution)/shard_map/ppermute | solution.py:387
  28.0 1.3 %collective-permute-start.5 = (bf16[96,256]{1,0:T(8,128)(2,1)S(1)}, bf16[96,256]{1,0:T(8,128)(2,1)S(1)}, u32[]{:S(2)}, u32[]{:S(2)}) collective-permute-start(bf16[96,256]{1,0:T(8,128)(2,1)S(1)} %get-tuple-element.40), channel_id=1, source_target_pairs={{0,48},{16,32},{32,16},{48,0},{64,112},{80,96},{96,80},{112,64},{1... | collective-permute-start | bytes 147464 | tf_op jit(solution)/shard_map/ppermute | solution.py:387
  29.3 3.0 %collective-permute-done.7.got2 = bf16[400,256]{1,0:T(8,128)(2,1)S(1)} collective-permute-done((bf16[400,256]{1,0:T(8,128)(2,1)}, bf16[400,256]{1,0:T(8,128)(2,1)S(1)}, u32[]{:S(2)}, u32[]{:S(2)}) %collective-permute-start.7) | collective-permute-done | bytes 204832 | tf_op jit(solution)/shard_map/ppermute | solution.py:383
  32.3 2.4 %collective-permute-done.8.got3 = bf16[400,256]{1,0:T(8,128)(2,1)S(1)} collective-permute-done((bf16[400,256]{1,0:T(8,128)(2,1)}, bf16[400,256]{1,0:T(8,128)(2,1)S(1)}, u32[]{:S(2)}, u32[]{:S(2)}) %collective-permute-start.8) | collective-permute-done | bytes 204832 | tf_op jit(solution)/shard_map/ppermute | solution.py:383
  34.8 1.0 %copy-done.2 = f32[384,256]{1,0:T(8,128)S(1)} copy-done((f32[384,256]{1,0:T(8,128)S(1)}, f32[384,256]{1,0:T(8,128)}, u32[]{:S(2)}) %copy-start.2) | copy-done | bytes 393240
  35.9 3.4 %collective-permute-start.10 = (bf16[96,256]{1,0:T(8,128)(2,1)S(1)}, bf16[96,256]{1,0:T(8,128)(2,1)S(1)}, u32[]{:S(2)}, u32[]{:S(2)}) collective-permute-start(bf16[96,256]{1,0:T(8,128)(2,1)S(1)} %get-tuple-element.47), channel_id=1, source_target_pairs={{0,32},{16,48},{32,0},{48,16},{64,96},{80,112},{96,64},{112,80},{1... | collective-permute-start | bytes 147464 | tf_op jit(solution)/shard_map/ppermute | solution.py:387
  39.4 2.8 %collective-permute-start.15 = (bf16[3,2,16,256]{3,2,1,0:T(8,128)(2,1)S(1)}, bf16[3,2,16,256]{3,2,1,0:T(8,128)(2,1)S(1)}, u32[]{:S(2)}, u32[]{:S(2)}) collective-permute-start(bf16[3,2,16,256]{3,2,1,0:T(8,128)(2,1)S(1)} %bitcast.20), channel_id=1, source_target_pairs={{0,6},{1,7},{2,4},{3,5},{4,2},{5,3},{6,0},{7,1},{8,14},{9,15},{10,... | collective-permute-start | bytes 147464 | tf_op jit(solution)/shard_map/ppermute | solution.py:408
  43.7 1.6 %collective-permute-done.15 = bf16[3,2,16,256]{3,2,1,0:T(8,128)(2,1)S(1)} collective-permute-done((bf16[3,2,16,256]{3,2,1,0:T(8,128)(2,1)S(1)}, bf16[3,2,16,256]{3,2,1,0:T(8,128)(2,1)S(1)}, u32[]{:S(2)}, u32[]{:S(2)}) %collective-permute-start.15) | collective-permute-done | bytes 49184 | tf_op jit(solution)/shard_map/ppermute | solution.py:408
  45.3 1.6 %collective-permute-start.9 = (bf16[96,256]{1,0:T(8,128)(2,1)S(1)}, bf16[96,256]{1,0:T(8,128)(2,1)S(1)}, u32[]{:S(2)}, u32[]{:S(2)}) collective-permute-start(bf16[96,256]{1,0:T(8,128)(2,1)S(1)} %get-tuple-element.46), channel_id=1, source_target_pairs={{0,16},{16,0},{32,48},{48,32},{64,80},{80,64},{96,112},{112,96},{1... | collective-permute-start | bytes 147464 | tf_op jit(solution)/shard_map/ppermute | solution.py:387
  47.9 5.6 %collective-permute-start.18 = (bf16[3,2,16,256]{3,2,1,0:T(8,128)(2,1)S(1)}, bf16[3,2,16,256]{3,2,1,0:T(8,128)(2,1)S(1)}, u32[]{:S(2)}, u32[]{:S(2)}) collective-permute-start(bf16[3,2,16,256]{3,2,1,0:T(8,128)(2,1)S(1)} %select_select_fusion), channel_id=1, source_target_pairs={{0,40},{1,41},{2,42},{3,43},{4,44},{5,45},{6,46},{7,47},{8,32},{9,... | collective-permute-start | bytes 147464 | tf_op jit(solution)/shard_map/ppermute | solution.py:410
  53.6 2.1 %collective-permute-done.18 = bf16[3,2,16,256]{3,2,1,0:T(8,128)(2,1)S(1)} collective-permute-done((bf16[3,2,16,256]{3,2,1,0:T(8,128)(2,1)S(1)}, bf16[3,2,16,256]{3,2,1,0:T(8,128)(2,1)S(1)}, u32[]{:S(2)}, u32[]{:S(2)}) %collective-permute-start.18) | collective-permute-done | bytes 49184 | tf_op jit(solution)/shard_map/ppermute | solution.py:410
  55.8 1.2 %collective-permute-done.19 = bf16[3,2,16,256]{3,2,1,0:T(8,128)(2,1)S(1)} collective-permute-done((bf16[3,2,16,256]{3,2,1,0:T(8,128)(2,1)S(1)}, bf16[3,2,16,256]{3,2,1,0:T(8,128)(2,1)S(1)}, u32[]{:S(2)}, u32[]{:S(2)}) %collective-permute-start.19) | collective-permute-done | bytes 49184 | tf_op jit(solution)/shard_map/ppermute | solution.py:412
  57.2 2.8 %collective-permute-start.21 = (bf16[3,2,16,256]{3,2,1,0:T(8,128)(2,1)S(1)}, bf16[3,2,16,256]{3,2,1,0:T(8,128)(2,1)S(1)}, u32[]{:S(2)}, u32[]{:S(2)}) collective-permute-start(bf16[3,2,16,256]{3,2,1,0:T(8,128)(2,1)S(1)} %broadcast_select_fusion.1.p0), channel_id=1, source_target_pairs={{0,32},{16,48},{32,0},{48,16},{64,96},{80,112},{96,64},{112,80},{1... | collective-permute-start | bytes 147464 | tf_op jit(solution)/shard_map/ppermute | solution.py:387
  61.6 1.7 %collective-permute-done.21.p2 = bf16[3,2,16,256]{3,2,1,0:T(8,128)(2,1)S(1)} collective-permute-done((bf16[3,2,16,256]{3,2,1,0:T(8,128)(2,1)S(1)}, bf16[3,2,16,256]{3,2,1,0:T(8,128)(2,1)S(1)}, u32[]{:S(2)}, u32[]{:S(2)}) %collective-permute-start.21) | collective-permute-done | bytes 49184 | tf_op jit(solution)/shard_map/ppermute | solution.py:387
  63.3 2.0 %collective-permute-done.22.p3 = bf16[3,2,16,256]{3,2,1,0:T(8,128)(2,1)S(1)} collective-permute-done((bf16[3,2,16,256]{3,2,1,0:T(8,128)(2,1)S(1)}, bf16[3,2,16,256]{3,2,1,0:T(8,128)(2,1)S(1)}, u32[]{:S(2)}, u32[]{:S(2)}) %collective-permute-start.22) | collective-permute-done | bytes 49184 | tf_op jit(solution)/shard_map/ppermute | solution.py:387
  66.0 1.0 %collective-permute-start.12 = (bf16[6,2,16,256]{3,2,1,0:T(8,128)(2,1)S(1)}, bf16[6,2,16,256]{3,2,1,0:T(8,128)(2,1)S(1)}, u32[]{:S(2)}, u32[]{:S(2)}) collective-permute-start(bf16[6,2,16,256]{3,2,1,0:T(8,128)(2,1)S(1)} %pad_maximum_fusion.p0), channel_id=1, source_target_pairs={{0,16},{16,0},{32,48},{48,32},{64,80},{80,64},{96,112},{112,96},{1... | collective-permute-start | bytes 294920 | tf_op jit(solution)/shard_map/ppermute | solution.py:387
  67.0 1.8 %collective-permute-start.13 = (bf16[6,2,16,256]{3,2,1,0:T(8,128)(2,1)S(1)}, bf16[6,2,16,256]{3,2,1,0:T(8,128)(2,1)S(1)}, u32[]{:S(2)}, u32[]{:S(2)}) collective-permute-start(bf16[6,2,16,256]{3,2,1,0:T(8,128)(2,1)S(1)} %pad_maximum_fusion.p0), channel_id=1, source_target_pairs={{0,32},{16,48},{32,0},{48,16},{64,96},{80,112},{96,64},{112,80},{1... | collective-permute-start | bytes 294920 | tf_op jit(solution)/shard_map/ppermute | solution.py:387
  69.6 1.8 %collective-permute-start.27 = (bf16[2,4,2,16,256]{4,3,2,1,0:T(8,128)(2,1)S(1)}, bf16[2,4,2,16,256]{4,3,2,1,0:T(8,128)(2,1)S(1)}, u32[]{:S(2)}, u32[]{:S(2)}) collective-permute-start(bf16[2,4,2,16,256]{4,3,2,1,0:T(8,128)(2,1)S(1)} %get-tuple-element.51), channel_id=1, source_target_pairs={{0,128},{16,144},{32,160},{48,176},{64,192},{80,208},{96,224},{112... | collective-permute-start | bytes 393224 | tf_op jit(solution)/shard_map/ppermute | solution.py:383
  71.8 2.5 %collective-permute-start.28 = (bf16[2,4,2,16,256]{4,3,2,1,0:T(8,128)(2,1)S(1)}, bf16[2,4,2,16,256]{4,3,2,1,0:T(8,128)(2,1)S(1)}, u32[]{:S(2)}, u32[]{:S(2)}) collective-permute-start(bf16[2,4,2,16,256]{4,3,2,1,0:T(8,128)(2,1)S(1)} %get-tuple-element.52), channel_id=1, source_target_pairs={{0,192},{16,208},{32,224},{48,240},{64,128},{80,144},{96,160},{112... | collective-permute-start | bytes 393224 | tf_op jit(solution)/shard_map/ppermute | solution.py:383
  75.3 2.6 %collective-permute-done.14.p3 = bf16[6,2,16,256]{3,2,1,0:T(8,128)(2,1)S(1)} collective-permute-done((bf16[6,2,16,256]{3,2,1,0:T(8,128)(2,1)S(1)}, bf16[6,2,16,256]{3,2,1,0:T(8,128)(2,1)S(1)}, u32[]{:S(2)}, u32[]{:S(2)}) %collective-permute-start.14) | collective-permute-done | bytes 98336 | tf_op jit(solution)/shard_map/ppermute | solution.py:387
  78.5 1.8 %collective-permute-start.23 = (bf16[2,4,2,16,256]{4,3,2,1,0:T(8,128)(2,1)S(1)}, bf16[2,4,2,16,256]{4,3,2,1,0:T(8,128)(2,1)S(1)}, u32[]{:S(2)}, u32[]{:S(2)}) collective-permute-start(bf16[2,4,2,16,256]{4,3,2,1,0:T(8,128)(2,1)S(1)} %get-tuple-element.58), channel_id=1, source_target_pairs={{0,64},{16,80},{32,96},{48,112},{64,0},{80,16},{96,32},{112,48},{1... | collective-permute-start | bytes 393224 | tf_op jit(solution)/shard_map/ppermute | solution.py:383
  80.4 2.9 %collective-permute-start.25 = (bf16[2,4,2,16,256]{4,3,2,1,0:T(8,128)(2,1)S(1)}, bf16[2,4,2,16,256]{4,3,2,1,0:T(8,128)(2,1)S(1)}, u32[]{:S(2)}, u32[]{:S(2)}) collective-permute-start(bf16[2,4,2,16,256]{4,3,2,1,0:T(8,128)(2,1)S(1)} %get-tuple-element.60), channel_id=1, source_target_pairs={{0,192},{16,208},{32,224},{48,240},{64,128},{80,144},{96,160},{112... | collective-permute-start | bytes 393224 | tf_op jit(solution)/shard_map/ppermute | solution.py:383
  83.3 2.2 %copy-done = bf16[2,2,1024,512]{3,2,1,0:T(8,128)(2,1)S(1)} copy-done((bf16[2,2,1024,512]{3,2,1,0:T(8,128)(2,1)S(1)}, bf16[2,2,1024,512]{3,2,1,0:T(8,128)(2,1)}, u32[]{:S(2)}) %copy-start) | copy-done | bytes 4194328
  85.5 2.2 %transpose_tau.1.tt_ref = bf16[2,512,2048]{2,1,0:T(8,128)(2,1)S(1)} custom-call(bf16[2,2,4,256,512]{4,3,2,1,0:T(8,128)(2,1)S(1)} %bitcast.16), custom_call_target="tpu_custom_call" | custom-call | tf_op jit(solution)/shard_map/transpose_tau/pallas_call | solution.py:213
  87.8 7.0 %middle.1.m_ref = bf16[2,512,1024]{2,1,0:T(8,128)(2,1)S(1)} custom-call(s32[1]{0:T(128)} %copy.8.source, bf16[2,4,2,16,256]{4,3,2,1,0:T(8,128)(2,1)S(1)} %get-tuple-element.49.f0, bf16[2,4,2,16,256]{4,3,2,1,0:T(8,128)(2,1)S(1)} %collective-permute-done.26.f1, bf16[2,4,2,16,256]{4,3,2,1,0:T(8,128)(2,1)S(1)} %collective-permute-done.27.f2, ...), custom_call_target="tpu_custom_call" | custom-call | tf_op jit(solution)/shard_map/middle/pallas_call | solution.py:286
  94.8 3.3 %outer.1 = bf16[2,2,512,512]{3,2,1,0:T(8,128)(2,1)} custom-call(s32[4]{0:T(128)S(1)} %copy-done.4, bf16[2,4,2,16,256]{4,3,2,1,0:T(8,128)(2,1)S(1)} %get-tuple-element.57.s0, bf16[2,4,2,16,256]{4,3,2,1,0:T(8,128)(2,1)S(1)} %collective-permute-done.23.s1, bf16[2,4,2,16,256]{4,3,2,1,0:T(8,128)(2,1)S(1)} %collective-permute-done.24.s2, ...), custom_call_target="tpu_custom_call" | custom-call | tf_op jit(solution)/shard_map/outer/pallas_call | solution.py:350
  (60 shorter events, 9.6 us)
Async XLA Ops:
  0.7 23.2 %copy-start.5 = (s32[2]{0:T(128)S(1)}, s32[2]{0:T(128)}, u32[]{:S(2)}) copy-start(s32[2]{0:T(128)} %slices.3) | copy-start | bytes 28
  0.7 23.2 %copy-start.6 = (s32[2]{0:T(128)S(1)}, s32[2]{0:T(128)}, u32[]{:S(2)}) copy-start(s32[2]{0:T(128)} %moments.3) | copy-start | bytes 28
  7.6 16.6 %copy-start.3 = (f32[384,256]{1,0:T(8,128)S(1)}, f32[384,256]{1,0:T(8,128)}, u32[]{:S(2)}) copy-start(f32[384,256]{1,0:T(8,128)} %get-tuple-element.36.kept) | copy-start | bytes 1179652
  7.6 16.1 %collective-permute-start = (bf16[400,256]{1,0:T(8,128)(2,1)}, bf16[400,256]{1,0:T(8,128)(2,1)S(1)}, u32[]{:S(2)}, u32[]{:S(2)}) collective-permute-start(bf16[400,256]{1,0:T(8,128)(2,1)} %get-tuple-element.33), channel_id=1, source_target_pairs={{0,64},{16,80},{32,96},{48,112},{64,0},{80,16},{96,32},{112,48},{1... | collective-permute-start | bytes 614408 | tf_op jit(solution)/shard_map/ppermute | solution.py:383
  9.2 14.7 %collective-permute-start.1 = (bf16[400,256]{1,0:T(8,128)(2,1)}, bf16[400,256]{1,0:T(8,128)(2,1)S(1)}, u32[]{:S(2)}, u32[]{:S(2)}) collective-permute-start(bf16[400,256]{1,0:T(8,128)(2,1)} %get-tuple-element.34), channel_id=1, source_target_pairs={{0,128},{16,144},{32,160},{48,176},{64,192},{80,208},{96,224},{112... | collective-permute-start | bytes 614408 | tf_op jit(solution)/shard_map/ppermute | solution.py:383
  12.1 12.1 %collective-permute-start.2 = (bf16[400,256]{1,0:T(8,128)(2,1)}, bf16[400,256]{1,0:T(8,128)(2,1)S(1)}, u32[]{:S(2)}, u32[]{:S(2)}) collective-permute-start(bf16[400,256]{1,0:T(8,128)(2,1)} %get-tuple-element.35), channel_id=1, source_target_pairs={{0,192},{16,208},{32,224},{48,240},{64,128},{80,144},{96,160},{112... | collective-permute-start | bytes 614408 | tf_op jit(solution)/shard_map/ppermute | solution.py:383
  19.1 8.8 %collective-permute-start.6 = (bf16[400,256]{1,0:T(8,128)(2,1)}, bf16[400,256]{1,0:T(8,128)(2,1)S(1)}, u32[]{:S(2)}, u32[]{:S(2)}) collective-permute-start(bf16[400,256]{1,0:T(8,128)(2,1)} %get-tuple-element.42), channel_id=1, source_target_pairs={{0,64},{16,80},{32,96},{48,112},{64,0},{80,16},{96,32},{112,48},{1... | collective-permute-start | bytes 614408 | tf_op jit(solution)/shard_map/ppermute | solution.py:383
  19.6 12.8 %collective-permute-start.7 = (bf16[400,256]{1,0:T(8,128)(2,1)}, bf16[400,256]{1,0:T(8,128)(2,1)S(1)}, u32[]{:S(2)}, u32[]{:S(2)}) collective-permute-start(bf16[400,256]{1,0:T(8,128)(2,1)} %get-tuple-element.43), channel_id=1, source_target_pairs={{0,128},{16,144},{32,160},{48,176},{64,192},{80,208},{96,224},{112... | collective-permute-start | bytes 614408 | tf_op jit(solution)/shard_map/ppermute | solution.py:383
  23.7 11.1 %collective-permute-start.8 = (bf16[400,256]{1,0:T(8,128)(2,1)}, bf16[400,256]{1,0:T(8,128)(2,1)S(1)}, u32[]{:S(2)}, u32[]{:S(2)}) collective-permute-start(bf16[400,256]{1,0:T(8,128)(2,1)} %get-tuple-element.44), channel_id=1, source_target_pairs={{0,192},{16,208},{32,224},{48,240},{64,128},{80,144},{96,160},{112... | collective-permute-start | bytes 614408 | tf_op jit(solution)/shard_map/ppermute | solution.py:383
  24.3 15.0 %collective-permute-start.3 = (bf16[96,256]{1,0:T(8,128)(2,1)S(1)}, bf16[96,256]{1,0:T(8,128)(2,1)S(1)}, u32[]{:S(2)}, u32[]{:S(2)}) collective-permute-start(bf16[96,256]{1,0:T(8,128)(2,1)S(1)} %get-tuple-element.38), channel_id=1, source_target_pairs={{0,16},{16,0},{32,48},{48,32},{64,80},{80,64},{96,112},{112,96},{1... | collective-permute-start | bytes 147464 | tf_op jit(solution)/shard_map/ppermute | solution.py:387
  26.1 13.2 %collective-permute-start.4 = (bf16[96,256]{1,0:T(8,128)(2,1)S(1)}, bf16[96,256]{1,0:T(8,128)(2,1)S(1)}, u32[]{:S(2)}, u32[]{:S(2)}) collective-permute-start(bf16[96,256]{1,0:T(8,128)(2,1)S(1)} %get-tuple-element.39), channel_id=1, source_target_pairs={{0,32},{16,48},{32,0},{48,16},{64,96},{80,112},{96,64},{112,80},{1... | collective-permute-start | bytes 147464 | tf_op jit(solution)/shard_map/ppermute | solution.py:387
  28.0 11.4 %collective-permute-start.5 = (bf16[96,256]{1,0:T(8,128)(2,1)S(1)}, bf16[96,256]{1,0:T(8,128)(2,1)S(1)}, u32[]{:S(2)}, u32[]{:S(2)}) collective-permute-start(bf16[96,256]{1,0:T(8,128)(2,1)S(1)} %get-tuple-element.40), channel_id=1, source_target_pairs={{0,48},{16,32},{32,16},{48,0},{64,112},{80,96},{96,80},{112,64},{1... | collective-permute-start | bytes 147464 | tf_op jit(solution)/shard_map/ppermute | solution.py:387
  35.9 24.1 %collective-permute-start.10 = (bf16[96,256]{1,0:T(8,128)(2,1)S(1)}, bf16[96,256]{1,0:T(8,128)(2,1)S(1)}, u32[]{:S(2)}, u32[]{:S(2)}) collective-permute-start(bf16[96,256]{1,0:T(8,128)(2,1)S(1)} %get-tuple-element.47), channel_id=1, source_target_pairs={{0,32},{16,48},{32,0},{48,16},{64,96},{80,112},{96,64},{112,80},{1... | collective-permute-start | bytes 147464 | tf_op jit(solution)/shard_map/ppermute | solution.py:387
  39.2 21.4 %collective-permute-start.11 = (bf16[96,256]{1,0:T(8,128)(2,1)S(1)}, bf16[96,256]{1,0:T(8,128)(2,1)S(1)}, u32[]{:S(2)}, u32[]{:S(2)}) collective-permute-start(bf16[96,256]{1,0:T(8,128)(2,1)S(1)} %get-tuple-element.48), channel_id=1, source_target_pairs={{0,48},{16,32},{32,16},{48,0},{64,112},{80,96},{96,80},{112,64},{1... | collective-permute-start | bytes 147464 | tf_op jit(solution)/shard_map/ppermute | solution.py:387
  39.4 5.9 %collective-permute-start.15 = (bf16[3,2,16,256]{3,2,1,0:T(8,128)(2,1)S(1)}, bf16[3,2,16,256]{3,2,1,0:T(8,128)(2,1)S(1)}, u32[]{:S(2)}, u32[]{:S(2)}) collective-permute-start(bf16[3,2,16,256]{3,2,1,0:T(8,128)(2,1)S(1)} %bitcast.20), channel_id=1, source_target_pairs={{0,6},{1,7},{2,4},{3,5},{4,2},{5,3},{6,0},{7,1},{8,14},{9,15},{10,... | collective-permute-start | bytes 147464 | tf_op jit(solution)/shard_map/ppermute | solution.py:408
  42.2 5.6 %collective-permute-start.16 = (bf16[3,2,16,256]{3,2,1,0:T(8,128)(2,1)S(1)}, bf16[3,2,16,256]{3,2,1,0:T(8,128)(2,1)S(1)}, u32[]{:S(2)}, u32[]{:S(2)}) collective-permute-start(bf16[3,2,16,256]{3,2,1,0:T(8,128)(2,1)S(1)} %bitcast.21), channel_id=1, source_target_pairs={{0,4},{1,5},{2,6},{3,7},{4,0},{5,1},{6,2},{7,3},{8,12},{9,13},{10,... | collective-permute-start | bytes 147464 | tf_op jit(solution)/shard_map/ppermute | solution.py:408
  43.0 4.8 %collective-permute-start.17 = (bf16[3,2,16,256]{3,2,1,0:T(8,128)(2,1)S(1)}, bf16[3,2,16,256]{3,2,1,0:T(8,128)(2,1)S(1)}, u32[]{:S(2)}, u32[]{:S(2)}) collective-permute-start(bf16[3,2,16,256]{3,2,1,0:T(8,128)(2,1)S(1)} %bitcast.22), channel_id=1, source_target_pairs={{0,2},{1,3},{2,0},{3,1},{4,6},{5,7},{6,4},{7,5},{8,10},{9,11},{10,... | collective-permute-start | bytes 147464 | tf_op jit(solution)/shard_map/ppermute | solution.py:408
  45.3 15.3 %collective-permute-start.9 = (bf16[96,256]{1,0:T(8,128)(2,1)S(1)}, bf16[96,256]{1,0:T(8,128)(2,1)S(1)}, u32[]{:S(2)}, u32[]{:S(2)}) collective-permute-start(bf16[96,256]{1,0:T(8,128)(2,1)S(1)} %get-tuple-element.46), channel_id=1, source_target_pairs={{0,16},{16,0},{32,48},{48,32},{64,80},{80,64},{96,112},{112,96},{1... | collective-permute-start | bytes 147464 | tf_op jit(solution)/shard_map/ppermute | solution.py:387
  47.9 7.8 %collective-permute-start.18 = (bf16[3,2,16,256]{3,2,1,0:T(8,128)(2,1)S(1)}, bf16[3,2,16,256]{3,2,1,0:T(8,128)(2,1)S(1)}, u32[]{:S(2)}, u32[]{:S(2)}) collective-permute-start(bf16[3,2,16,256]{3,2,1,0:T(8,128)(2,1)S(1)} %select_select_fusion), channel_id=1, source_target_pairs={{0,40},{1,41},{2,42},{3,43},{4,44},{5,45},{6,46},{7,47},{8,32},{9,... | collective-permute-start | bytes 147464 | tf_op jit(solution)/shard_map/ppermute | solution.py:410
  55.7 1.3 %collective-permute-start.19 = (bf16[3,2,16,256]{3,2,1,0:T(8,128)(2,1)S(1)}, bf16[3,2,16,256]{3,2,1,0:T(8,128)(2,1)S(1)}, u32[]{:S(2)}, u32[]{:S(2)}) collective-permute-start(bf16[3,2,16,256]{3,2,1,0:T(8,128)(2,1)S(1)} %broadcast_select_fusion), channel_id=1, source_target_pairs={{0,1},{1,0},{2,3},{3,2},{4,5},{5,4},{6,7},{7,6},{8,9},{9,8},{10,11... | collective-permute-start | bytes 147464 | tf_op jit(solution)/shard_map/ppermute | solution.py:412
  57.0 4.6 %collective-permute-start.20 = (bf16[3,2,16,256]{3,2,1,0:T(8,128)(2,1)S(1)}, bf16[3,2,16,256]{3,2,1,0:T(8,128)(2,1)S(1)}, u32[]{:S(2)}, u32[]{:S(2)}) collective-permute-start(bf16[3,2,16,256]{3,2,1,0:T(8,128)(2,1)S(1)} %broadcast_select_fusion.1.p0), channel_id=1, source_target_pairs={{0,16},{16,0},{32,48},{48,32},{64,80},{80,64},{96,112},{112,96},{1... | collective-permute-start | bytes 147464 | tf_op jit(solution)/shard_map/ppermute | solution.py:387
  57.2 6.1 %collective-permute-start.21 = (bf16[3,2,16,256]{3,2,1,0:T(8,128)(2,1)S(1)}, bf16[3,2,16,256]{3,2,1,0:T(8,128)(2,1)S(1)}, u32[]{:S(2)}, u32[]{:S(2)}) collective-permute-start(bf16[3,2,16,256]{3,2,1,0:T(8,128)(2,1)S(1)} %broadcast_select_fusion.1.p0), channel_id=1, source_target_pairs={{0,32},{16,48},{32,0},{48,16},{64,96},{80,112},{96,64},{112,80},{1... | collective-permute-start | bytes 147464 | tf_op jit(solution)/shard_map/ppermute | solution.py:387
  59.9 5.3 %collective-permute-start.22 = (bf16[3,2,16,256]{3,2,1,0:T(8,128)(2,1)S(1)}, bf16[3,2,16,256]{3,2,1,0:T(8,128)(2,1)S(1)}, u32[]{:S(2)}, u32[]{:S(2)}) collective-permute-start(bf16[3,2,16,256]{3,2,1,0:T(8,128)(2,1)S(1)} %broadcast_select_fusion.1.p0), channel_id=1, source_target_pairs={{0,48},{16,32},{32,16},{48,0},{64,112},{80,96},{96,80},{112,64},{1... | collective-permute-start | bytes 147464 | tf_op jit(solution)/shard_map/ppermute | solution.py:387
  65.9 14.5 %collective-permute-start.26 = (bf16[2,4,2,16,256]{4,3,2,1,0:T(8,128)(2,1)S(1)}, bf16[2,4,2,16,256]{4,3,2,1,0:T(8,128)(2,1)S(1)}, u32[]{:S(2)}, u32[]{:S(2)}) collective-permute-start(bf16[2,4,2,16,256]{4,3,2,1,0:T(8,128)(2,1)S(1)} %get-tuple-element.50), channel_id=1, source_target_pairs={{0,64},{16,80},{32,96},{48,112},{64,0},{80,16},{96,32},{112,48},{1... | collective-permute-start | bytes 393224 | tf_op jit(solution)/shard_map/ppermute | solution.py:383
  66.0 5.8 %collective-permute-start.12 = (bf16[6,2,16,256]{3,2,1,0:T(8,128)(2,1)S(1)}, bf16[6,2,16,256]{3,2,1,0:T(8,128)(2,1)S(1)}, u32[]{:S(2)}, u32[]{:S(2)}) collective-permute-start(bf16[6,2,16,256]{3,2,1,0:T(8,128)(2,1)S(1)} %pad_maximum_fusion.p0), channel_id=1, source_target_pairs={{0,16},{16,0},{32,48},{48,32},{64,80},{80,64},{96,112},{112,96},{1... | collective-permute-start | bytes 294920 | tf_op jit(solution)/shard_map/ppermute | solution.py:387
  67.0 8.2 %collective-permute-start.13 = (bf16[6,2,16,256]{3,2,1,0:T(8,128)(2,1)S(1)}, bf16[6,2,16,256]{3,2,1,0:T(8,128)(2,1)S(1)}, u32[]{:S(2)}, u32[]{:S(2)}) collective-permute-start(bf16[6,2,16,256]{3,2,1,0:T(8,128)(2,1)S(1)} %pad_maximum_fusion.p0), channel_id=1, source_target_pairs={{0,32},{16,48},{32,0},{48,16},{64,96},{80,112},{96,64},{112,80},{1... | collective-permute-start | bytes 294920 | tf_op jit(solution)/shard_map/ppermute | solution.py:387
  68.8 9.1 %collective-permute-start.14 = (bf16[6,2,16,256]{3,2,1,0:T(8,128)(2,1)S(1)}, bf16[6,2,16,256]{3,2,1,0:T(8,128)(2,1)S(1)}, u32[]{:S(2)}, u32[]{:S(2)}) collective-permute-start(bf16[6,2,16,256]{3,2,1,0:T(8,128)(2,1)S(1)} %pad_maximum_fusion.p0), channel_id=1, source_target_pairs={{0,48},{16,32},{32,16},{48,0},{64,112},{80,96},{96,80},{112,64},{1... | collective-permute-start | bytes 294920 | tf_op jit(solution)/shard_map/ppermute | solution.py:387
  69.6 18.1 %collective-permute-start.27 = (bf16[2,4,2,16,256]{4,3,2,1,0:T(8,128)(2,1)S(1)}, bf16[2,4,2,16,256]{4,3,2,1,0:T(8,128)(2,1)S(1)}, u32[]{:S(2)}, u32[]{:S(2)}) collective-permute-start(bf16[2,4,2,16,256]{4,3,2,1,0:T(8,128)(2,1)S(1)} %get-tuple-element.51), channel_id=1, source_target_pairs={{0,128},{16,144},{32,160},{48,176},{64,192},{80,208},{96,224},{112... | collective-permute-start | bytes 393224 | tf_op jit(solution)/shard_map/ppermute | solution.py:383
  71.8 16.0 %collective-permute-start.28 = (bf16[2,4,2,16,256]{4,3,2,1,0:T(8,128)(2,1)S(1)}, bf16[2,4,2,16,256]{4,3,2,1,0:T(8,128)(2,1)S(1)}, u32[]{:S(2)}, u32[]{:S(2)}) collective-permute-start(bf16[2,4,2,16,256]{4,3,2,1,0:T(8,128)(2,1)S(1)} %get-tuple-element.52), channel_id=1, source_target_pairs={{0,192},{16,208},{32,224},{48,240},{64,128},{80,144},{96,160},{112... | collective-permute-start | bytes 393224 | tf_op jit(solution)/shard_map/ppermute | solution.py:383
  78.5 16.2 %collective-permute-start.23 = (bf16[2,4,2,16,256]{4,3,2,1,0:T(8,128)(2,1)S(1)}, bf16[2,4,2,16,256]{4,3,2,1,0:T(8,128)(2,1)S(1)}, u32[]{:S(2)}, u32[]{:S(2)}) collective-permute-start(bf16[2,4,2,16,256]{4,3,2,1,0:T(8,128)(2,1)S(1)} %get-tuple-element.58), channel_id=1, source_target_pairs={{0,64},{16,80},{32,96},{48,112},{64,0},{80,16},{96,32},{112,48},{1... | collective-permute-start | bytes 393224 | tf_op jit(solution)/shard_map/ppermute | solution.py:383
  80.3 14.4 %collective-permute-start.24 = (bf16[2,4,2,16,256]{4,3,2,1,0:T(8,128)(2,1)S(1)}, bf16[2,4,2,16,256]{4,3,2,1,0:T(8,128)(2,1)S(1)}, u32[]{:S(2)}, u32[]{:S(2)}) collective-permute-start(bf16[2,4,2,16,256]{4,3,2,1,0:T(8,128)(2,1)S(1)} %get-tuple-element.59), channel_id=1, source_target_pairs={{0,128},{16,144},{32,160},{48,176},{64,192},{80,208},{96,224},{112... | collective-permute-start | bytes 393224 | tf_op jit(solution)/shard_map/ppermute | solution.py:383
  80.4 14.3 %collective-permute-start.25 = (bf16[2,4,2,16,256]{4,3,2,1,0:T(8,128)(2,1)S(1)}, bf16[2,4,2,16,256]{4,3,2,1,0:T(8,128)(2,1)S(1)}, u32[]{:S(2)}, u32[]{:S(2)}) collective-permute-start(bf16[2,4,2,16,256]{4,3,2,1,0:T(8,128)(2,1)S(1)} %get-tuple-element.60), channel_id=1, source_target_pairs={{0,192},{16,208},{32,224},{48,240},{64,128},{80,144},{96,160},{112... | collective-permute-start | bytes 393224 | tf_op jit(solution)/shard_map/ppermute | solution.py:383
  (4 other events, 12.5 us)

commit v2 on v1

--- a/solution.py
+++ b/solution.py
@@ -316,16 +316,20 @@
     site = lax.axis_index("site")
     my_y = site // ZN
     my_z = site % ZN
-    for dy, s_ref in enumerate((s0, s1, s2, s3)):
-        for dz in range(ZN):
-            first = first_row(my_y, my_z, dy, dz)
-            s_re = s_ref[k, dz, 0]
-            s_im = s_ref[k, dz, 1]
-            smat[pl.ds(first, rows), :NVEC] = s_re
-            smat[pl.ds(first, rows), NVEC:] = s_im
-            smat[pl.ds(NVEC + first, rows), :NVEC] = -s_im
-            smat[pl.ds(NVEC + first, rows), NVEC:] = s_re
-    wide = m_ref.shape[1]
+
+    @pl.when(pl.program_id(1) == 0)
+    def _():
+        for dy, s_ref in enumerate((s0, s1, s2, s3)):
+            for dz in range(ZN):
+                first = first_row(my_y, my_z, dy, dz)
+                s_re = s_ref[k, dz, 0]
+                s_im = s_ref[k, dz, 1]
+                smat[pl.ds(first, rows), :NVEC] = s_re
+                smat[pl.ds(first, rows), NVEC:] = s_im
+                smat[pl.ds(NVEC + first, rows), :NVEC] = -s_im
+                smat[pl.ds(NVEC + first, rows), NVEC:] = s_re
+
+    wide = m_ref.shape[2] // 2
     s_all = smat[...]
     inner = []
     for e in range(2):
@@ -351,10 +355,10 @@
         outer_kernel,
         grid_spec=pltpu.PrefetchScalarGridSpec(
             num_scalar_prefetch=1,
-            grid=(count,),
+            grid=(count, 2),
             in_specs=[s_spec() for _ in range(4)]
-            + [pl.BlockSpec((1, wide, 2 * wide), lambda k, *_: (k, 0, 0))],
-            out_specs=pl.BlockSpec((1, 2, wide, wide), lambda k, *_: (k, 0, 0, 0)),
+            + [pl.BlockSpec((1, wide // 2, 2 * wide), lambda k, j, *_: (k, j, 0))],
+            out_specs=pl.BlockSpec((1, 2, wide // 2, wide), lambda k, j, *_: (k, 0, j, 0)),
             scratch_shapes=[pltpu.VMEM((2 * NVEC, 2 * NVEC), BF16)],
         ),
         out_shape=jax.ShapeDtypeStruct((count, 2, wide, wide), BF16),

time: 98.3 us -> 98.8 us (level)
  no operation moved by 1% of the time
where the time goes in v2:
time: 98.8 us; the launch traced here: 98.5 us
  starting transfers between devices  45.6 us (46%)
  Pallas kernels  27.9 us (28%)
  waiting for transfers between devices  20.4 us (21%)
  local copies, waits for them, and re-layouts  3.21 us (3%)
    ppermute x12, starting transfers between devices, swap_y(): got[step] = lax.ppermute(parts[step], 'site', y_swap(step))  18.7 us
    ppermute x12, starting transfers between devices, swap_z(): lax.ppermute(parts[step], 'site', z_swap(step))  17 us
    pallas_call x2, Pallas kernels, partial_elementals(): pl.pallas_call(functools.partial(elementals_kernel, turned), in_specs=[sm...  13.6 us
    ppermute x12, waiting for transfers between devices, swap_z(): lax.ppermute(parts[step], 'site', z_swap(step))  8.72 us
    pallas_call x1, Pallas kernels, middle_of(): pl.pallas_call(middle_kernel, grid_spec=pltpu.PrefetchScalarGridSpec(num_...  6.96 us
    ppermute x12, waiting for transfers between devices, swap_y(): got[step] = lax.ppermute(parts[step], 'site', y_swap(step))  5.8 us
    ppermute x1, starting transfers between devices, body(): got = lax.ppermute(held, ('site', 'cuts'), half_swap())  5.58 us
    ppermute x3, starting transfers between devices, body(): got = lax.ppermute(chunk_a, 'cuts', cut_swap(step, 0))  4.18 us
  transfers between devices with their start and end apart: 29, of which 13 were waited for; matrix products, arithmetic and copies ran while one was open for 0% of the time, Pallas kernels for 17%

profile of v2, /device:TPU:32, one launch (start us, length us, event | category | flops | bytes accessed | tf_op | source)
XLA Modules:
  0.0 98.5 jit_solution(5406055640142120657)
XLA Ops:
  0.7 6.9 %elementals.2 = (f32[384,256]{1,0:T(8,128)}, bf16[400,256]{1,0:T(8,128)(2,1)}, bf16[400,256]{1,0:T(8,128)(2,1)}, bf16[400,256]{1,0:T(8,128)(2,1)}) custom-call(s32[1]{0:T(128)} %copy.8.source, s32[3,3]{1,0:T(4,128)} %mom.3, s32[2]{0:T(128)} %slices.3, s32[2]{0:T(128)} %moments.3, bf16[2,2,1728,256]{3,2,1,0:T(8,128)(2,1)} %bitcast.18), custom_call_target="tpu_custom_call" | custom-call | tf_op jit(solution)/shard_map/elementals/pallas_call | solution.py:160
  7.6 1.7 %collective-permute-start = (bf16[400,256]{1,0:T(8,128)(2,1)}, bf16[400,256]{1,0:T(8,128)(2,1)S(1)}, u32[]{:S(2)}, u32[]{:S(2)}) collective-permute-start(bf16[400,256]{1,0:T(8,128)(2,1)} %get-tuple-element.33), channel_id=1, source_target_pairs={{0,64},{16,80},{32,96},{48,112},{64,0},{80,16},{96,32},{112,48},{1... | collective-permute-start | bytes 614408 | tf_op jit(solution)/shard_map/ppermute | solution.py:387
  9.2 2.9 %collective-permute-start.1 = (bf16[400,256]{1,0:T(8,128)(2,1)}, bf16[400,256]{1,0:T(8,128)(2,1)S(1)}, u32[]{:S(2)}, u32[]{:S(2)}) collective-permute-start(bf16[400,256]{1,0:T(8,128)(2,1)} %get-tuple-element.34), channel_id=1, source_target_pairs={{0,128},{16,144},{32,160},{48,176},{64,192},{80,208},{96,224},{112... | collective-permute-start | bytes 614408 | tf_op jit(solution)/shard_map/ppermute | solution.py:387
  12.4 6.7 %elementals.3 = (f32[384,256]{1,0:T(8,128)}, bf16[400,256]{1,0:T(8,128)(2,1)}, bf16[400,256]{1,0:T(8,128)(2,1)}, bf16[400,256]{1,0:T(8,128)(2,1)}) custom-call(s32[1]{0:T(128)} %copy.8.source, s32[3,3]{1,0:T(4,128)} %mom.3, s32[2]{0:T(128)} %slices.3, s32[2]{0:T(128)} %moments.3, bf16[2,2,1728,256]{3,2,1,0:T(8,128)(2,1)} %bitcast.19), custom_call_target="tpu_custom_call" | custom-call | tf_op jit(solution)/shard_map/elementals/pallas_call | solution.py:160
  19.6 4.1 %collective-permute-start.7 = (bf16[400,256]{1,0:T(8,128)(2,1)}, bf16[400,256]{1,0:T(8,128)(2,1)S(1)}, u32[]{:S(2)}, u32[]{:S(2)}) collective-permute-start(bf16[400,256]{1,0:T(8,128)(2,1)} %get-tuple-element.43), channel_id=1, source_target_pairs={{0,128},{16,144},{32,160},{48,176},{64,192},{80,208},{96,224},{112... | collective-permute-start | bytes 614408 | tf_op jit(solution)/shard_map/ppermute | solution.py:387
  24.3 1.8 %collective-permute-start.3 = (bf16[96,256]{1,0:T(8,128)(2,1)S(1)}, bf16[96,256]{1,0:T(8,128)(2,1)S(1)}, u32[]{:S(2)}, u32[]{:S(2)}) collective-permute-start(bf16[96,256]{1,0:T(8,128)(2,1)S(1)} %get-tuple-element.38), channel_id=1, source_target_pairs={{0,16},{16,0},{32,48},{48,32},{64,80},{80,64},{96,112},{112,96},{1... | collective-permute-start | bytes 147464 | tf_op jit(solution)/shard_map/ppermute | solution.py:391
  26.1 1.8 %collective-permute-start.4 = (bf16[96,256]{1,0:T(8,128)(2,1)S(1)}, bf16[96,256]{1,0:T(8,128)(2,1)S(1)}, u32[]{:S(2)}, u32[]{:S(2)}) collective-permute-start(bf16[96,256]{1,0:T(8,128)(2,1)S(1)} %get-tuple-element.39), channel_id=1, source_target_pairs={{0,32},{16,48},{32,0},{48,16},{64,96},{80,112},{96,64},{112,80},{1... | collective-permute-start | bytes 147464 | tf_op jit(solution)/shard_map/ppermute | solution.py:391
  28.0 1.3 %collective-permute-start.5 = (bf16[96,256]{1,0:T(8,128)(2,1)S(1)}, bf16[96,256]{1,0:T(8,128)(2,1)S(1)}, u32[]{:S(2)}, u32[]{:S(2)}) collective-permute-start(bf16[96,256]{1,0:T(8,128)(2,1)S(1)} %get-tuple-element.40), channel_id=1, source_target_pairs={{0,48},{16,32},{32,16},{48,0},{64,112},{80,96},{96,80},{112,64},{1... | collective-permute-start | bytes 147464 | tf_op jit(solution)/shard_map/ppermute | solution.py:391
  29.3 3.0 %collective-permute-done.7.got2 = bf16[400,256]{1,0:T(8,128)(2,1)S(1)} collective-permute-done((bf16[400,256]{1,0:T(8,128)(2,1)}, bf16[400,256]{1,0:T(8,128)(2,1)S(1)}, u32[]{:S(2)}, u32[]{:S(2)}) %collective-permute-start.7) | collective-permute-done | bytes 204832 | tf_op jit(solution)/shard_map/ppermute | solution.py:387
  32.3 2.4 %collective-permute-done.8.got3 = bf16[400,256]{1,0:T(8,128)(2,1)S(1)} collective-permute-done((bf16[400,256]{1,0:T(8,128)(2,1)}, bf16[400,256]{1,0:T(8,128)(2,1)S(1)}, u32[]{:S(2)}, u32[]{:S(2)}) %collective-permute-start.8) | collective-permute-done | bytes 204832 | tf_op jit(solution)/shard_map/ppermute | solution.py:387
  34.8 1.0 %copy-done.2 = f32[384,256]{1,0:T(8,128)S(1)} copy-done((f32[384,256]{1,0:T(8,128)S(1)}, f32[384,256]{1,0:T(8,128)}, u32[]{:S(2)}) %copy-start.2) | copy-done | bytes 393240
  35.9 3.4 %collective-permute-start.10 = (bf16[96,256]{1,0:T(8,128)(2,1)S(1)}, bf16[96,256]{1,0:T(8,128)(2,1)S(1)}, u32[]{:S(2)}, u32[]{:S(2)}) collective-permute-start(bf16[96,256]{1,0:T(8,128)(2,1)S(1)} %get-tuple-element.47), channel_id=1, source_target_pairs={{0,32},{16,48},{32,0},{48,16},{64,96},{80,112},{96,64},{112,80},{1... | collective-permute-start | bytes 147464 | tf_op jit(solution)/shard_map/ppermute | solution.py:391
  39.4 2.8 %collective-permute-start.15 = (bf16[3,2,16,256]{3,2,1,0:T(8,128)(2,1)S(1)}, bf16[3,2,16,256]{3,2,1,0:T(8,128)(2,1)S(1)}, u32[]{:S(2)}, u32[]{:S(2)}) collective-permute-start(bf16[3,2,16,256]{3,2,1,0:T(8,128)(2,1)S(1)} %bitcast.20), channel_id=1, source_target_pairs={{0,6},{1,7},{2,4},{3,5},{4,2},{5,3},{6,0},{7,1},{8,14},{9,15},{10,... | collective-permute-start | bytes 147464 | tf_op jit(solution)/shard_map/ppermute | solution.py:412
  43.7 1.6 %collective-permute-done.15 = bf16[3,2,16,256]{3,2,1,0:T(8,128)(2,1)S(1)} collective-permute-done((bf16[3,2,16,256]{3,2,1,0:T(8,128)(2,1)S(1)}, bf16[3,2,16,256]{3,2,1,0:T(8,128)(2,1)S(1)}, u32[]{:S(2)}, u32[]{:S(2)}) %collective-permute-start.15) | collective-permute-done | bytes 49184 | tf_op jit(solution)/shard_map/ppermute | solution.py:412
  45.3 1.6 %collective-permute-start.9 = (bf16[96,256]{1,0:T(8,128)(2,1)S(1)}, bf16[96,256]{1,0:T(8,128)(2,1)S(1)}, u32[]{:S(2)}, u32[]{:S(2)}) collective-permute-start(bf16[96,256]{1,0:T(8,128)(2,1)S(1)} %get-tuple-element.46), channel_id=1, source_target_pairs={{0,16},{16,0},{32,48},{48,32},{64,80},{80,64},{96,112},{112,96},{1... | collective-permute-start | bytes 147464 | tf_op jit(solution)/shard_map/ppermute | solution.py:391
  47.9 5.6 %collective-permute-start.18 = (bf16[3,2,16,256]{3,2,1,0:T(8,128)(2,1)S(1)}, bf16[3,2,16,256]{3,2,1,0:T(8,128)(2,1)S(1)}, u32[]{:S(2)}, u32[]{:S(2)}) collective-permute-start(bf16[3,2,16,256]{3,2,1,0:T(8,128)(2,1)S(1)} %select_select_fusion), channel_id=1, source_target_pairs={{0,40},{1,41},{2,42},{3,43},{4,44},{5,45},{6,46},{7,47},{8,32},{9,... | collective-permute-start | bytes 147464 | tf_op jit(solution)/shard_map/ppermute | solution.py:414
  53.6 2.1 %collective-permute-done.18 = bf16[3,2,16,256]{3,2,1,0:T(8,128)(2,1)S(1)} collective-permute-done((bf16[3,2,16,256]{3,2,1,0:T(8,128)(2,1)S(1)}, bf16[3,2,16,256]{3,2,1,0:T(8,128)(2,1)S(1)}, u32[]{:S(2)}, u32[]{:S(2)}) %collective-permute-start.18) | collective-permute-done | bytes 49184 | tf_op jit(solution)/shard_map/ppermute | solution.py:414
  55.8 1.2 %collective-permute-done.19 = bf16[3,2,16,256]{3,2,1,0:T(8,128)(2,1)S(1)} collective-permute-done((bf16[3,2,16,256]{3,2,1,0:T(8,128)(2,1)S(1)}, bf16[3,2,16,256]{3,2,1,0:T(8,128)(2,1)S(1)}, u32[]{:S(2)}, u32[]{:S(2)}) %collective-permute-start.19) | collective-permute-done | bytes 49184 | tf_op jit(solution)/shard_map/ppermute | solution.py:416
  57.2 2.8 %collective-permute-start.21 = (bf16[3,2,16,256]{3,2,1,0:T(8,128)(2,1)S(1)}, bf16[3,2,16,256]{3,2,1,0:T(8,128)(2,1)S(1)}, u32[]{:S(2)}, u32[]{:S(2)}) collective-permute-start(bf16[3,2,16,256]{3,2,1,0:T(8,128)(2,1)S(1)} %broadcast_select_fusion.1.p0), channel_id=1, source_target_pairs={{0,32},{16,48},{32,0},{48,16},{64,96},{80,112},{96,64},{112,80},{1... | collective-permute-start | bytes 147464 | tf_op jit(solution)/shard_map/ppermute | solution.py:391
  61.6 1.7 %collective-permute-done.21.p2 = bf16[3,2,16,256]{3,2,1,0:T(8,128)(2,1)S(1)} collective-permute-done((bf16[3,2,16,256]{3,2,1,0:T(8,128)(2,1)S(1)}, bf16[3,2,16,256]{3,2,1,0:T(8,128)(2,1)S(1)}, u32[]{:S(2)}, u32[]{:S(2)}) %collective-permute-start.21) | collective-permute-done | bytes 49184 | tf_op jit(solution)/shard_map/ppermute | solution.py:391
  63.3 2.0 %collective-permute-done.22.p3 = bf16[3,2,16,256]{3,2,1,0:T(8,128)(2,1)S(1)} collective-permute-done((bf16[3,2,16,256]{3,2,1,0:T(8,128)(2,1)S(1)}, bf16[3,2,16,256]{3,2,1,0:T(8,128)(2,1)S(1)}, u32[]{:S(2)}, u32[]{:S(2)}) %collective-permute-start.22) | collective-permute-done | bytes 49184 | tf_op jit(solution)/shard_map/ppermute | solution.py:391
  66.0 1.0 %collective-permute-start.12 = (bf16[6,2,16,256]{3,2,1,0:T(8,128)(2,1)S(1)}, bf16[6,2,16,256]{3,2,1,0:T(8,128)(2,1)S(1)}, u32[]{:S(2)}, u32[]{:S(2)}) collective-permute-start(bf16[6,2,16,256]{3,2,1,0:T(8,128)(2,1)S(1)} %pad_maximum_fusion.p0), channel_id=1, source_target_pairs={{0,16},{16,0},{32,48},{48,32},{64,80},{80,64},{96,112},{112,96},{1... | collective-permute-start | bytes 294920 | tf_op jit(solution)/shard_map/ppermute | solution.py:391
  67.0 1.8 %collective-permute-start.13 = (bf16[6,2,16,256]{3,2,1,0:T(8,128)(2,1)S(1)}, bf16[6,2,16,256]{3,2,1,0:T(8,128)(2,1)S(1)}, u32[]{:S(2)}, u32[]{:S(2)}) collective-permute-start(bf16[6,2,16,256]{3,2,1,0:T(8,128)(2,1)S(1)} %pad_maximum_fusion.p0), channel_id=1, source_target_pairs={{0,32},{16,48},{32,0},{48,16},{64,96},{80,112},{96,64},{112,80},{1... | collective-permute-start | bytes 294920 | tf_op jit(solution)/shard_map/ppermute | solution.py:391
  69.6 1.8 %collective-permute-start.27 = (bf16[2,4,2,16,256]{4,3,2,1,0:T(8,128)(2,1)S(1)}, bf16[2,4,2,16,256]{4,3,2,1,0:T(8,128)(2,1)S(1)}, u32[]{:S(2)}, u32[]{:S(2)}) collective-permute-start(bf16[2,4,2,16,256]{4,3,2,1,0:T(8,128)(2,1)S(1)} %get-tuple-element.51), channel_id=1, source_target_pairs={{0,128},{16,144},{32,160},{48,176},{64,192},{80,208},{96,224},{112... | collective-permute-start | bytes 393224 | tf_op jit(solution)/shard_map/ppermute | solution.py:387
  71.8 2.5 %collective-permute-start.28 = (bf16[2,4,2,16,256]{4,3,2,1,0:T(8,128)(2,1)S(1)}, bf16[2,4,2,16,256]{4,3,2,1,0:T(8,128)(2,1)S(1)}, u32[]{:S(2)}, u32[]{:S(2)}) collective-permute-start(bf16[2,4,2,16,256]{4,3,2,1,0:T(8,128)(2,1)S(1)} %get-tuple-element.52), channel_id=1, source_target_pairs={{0,192},{16,208},{32,224},{48,240},{64,128},{80,144},{96,160},{112... | collective-permute-start | bytes 393224 | tf_op jit(solution)/shard_map/ppermute | solution.py:387
  75.3 2.6 %collective-permute-done.14.p3 = bf16[6,2,16,256]{3,2,1,0:T(8,128)(2,1)S(1)} collective-permute-done((bf16[6,2,16,256]{3,2,1,0:T(8,128)(2,1)S(1)}, bf16[6,2,16,256]{3,2,1,0:T(8,128)(2,1)S(1)}, u32[]{:S(2)}, u32[]{:S(2)}) %collective-permute-start.14) | collective-permute-done | bytes 98336 | tf_op jit(solution)/shard_map/ppermute | solution.py:391
  78.5 1.8 %collective-permute-start.23 = (bf16[2,4,2,16,256]{4,3,2,1,0:T(8,128)(2,1)S(1)}, bf16[2,4,2,16,256]{4,3,2,1,0:T(8,128)(2,1)S(1)}, u32[]{:S(2)}, u32[]{:S(2)}) collective-permute-start(bf16[2,4,2,16,256]{4,3,2,1,0:T(8,128)(2,1)S(1)} %get-tuple-element.58), channel_id=1, source_target_pairs={{0,64},{16,80},{32,96},{48,112},{64,0},{80,16},{96,32},{112,48},{1... | collective-permute-start | bytes 393224 | tf_op jit(solution)/shard_map/ppermute | solution.py:387
  80.4 2.9 %collective-permute-start.25 = (bf16[2,4,2,16,256]{4,3,2,1,0:T(8,128)(2,1)S(1)}, bf16[2,4,2,16,256]{4,3,2,1,0:T(8,128)(2,1)S(1)}, u32[]{:S(2)}, u32[]{:S(2)}) collective-permute-start(bf16[2,4,2,16,256]{4,3,2,1,0:T(8,128)(2,1)S(1)} %get-tuple-element.60), channel_id=1, source_target_pairs={{0,192},{16,208},{32,224},{48,240},{64,128},{80,144},{96,160},{112... | collective-permute-start | bytes 393224 | tf_op jit(solution)/shard_map/ppermute | solution.py:387
  83.3 2.2 %copy-done = bf16[2,2,1024,512]{3,2,1,0:T(8,128)(2,1)S(1)} copy-done((bf16[2,2,1024,512]{3,2,1,0:T(8,128)(2,1)S(1)}, bf16[2,2,1024,512]{3,2,1,0:T(8,128)(2,1)}, u32[]{:S(2)}) %copy-start) | copy-done | bytes 4194328
  85.5 2.2 %transpose_tau.1.tt_ref = bf16[2,512,2048]{2,1,0:T(8,128)(2,1)S(1)} custom-call(bf16[2,2,4,256,512]{4,3,2,1,0:T(8,128)(2,1)S(1)} %bitcast.16), custom_call_target="tpu_custom_call" | custom-call | tf_op jit(solution)/shard_map/transpose_tau/pallas_call | solution.py:213
  87.8 7.0 %middle.1.m_ref = bf16[2,512,1024]{2,1,0:T(8,128)(2,1)S(1)} custom-call(s32[1]{0:T(128)} %copy.8.source, bf16[2,4,2,16,256]{4,3,2,1,0:T(8,128)(2,1)S(1)} %get-tuple-element.49.f0, bf16[2,4,2,16,256]{4,3,2,1,0:T(8,128)(2,1)S(1)} %collective-permute-done.26.f1, bf16[2,4,2,16,256]{4,3,2,1,0:T(8,128)(2,1)S(1)} %collective-permute-done.27.f2, ...), custom_call_target="tpu_custom_call" | custom-call | tf_op jit(solution)/shard_map/middle/pallas_call | solution.py:286
  94.8 3.7 %outer.1 = bf16[2,2,512,512]{3,2,1,0:T(8,128)(2,1)} custom-call(s32[4]{0:T(128)S(1)} %copy-done.4, bf16[2,4,2,16,256]{4,3,2,1,0:T(8,128)(2,1)S(1)} %get-tuple-element.57.s0, bf16[2,4,2,16,256]{4,3,2,1,0:T(8,128)(2,1)S(1)} %collective-permute-done.23.s1, bf16[2,4,2,16,256]{4,3,2,1,0:T(8,128)(2,1)S(1)} %collective-permute-done.24.s2, ...), custom_call_target="tpu_custom_call" | custom-call | tf_op jit(solution)/shard_map/outer/pallas_call | solution.py:354
  (60 shorter events, 9.6 us)
Async XLA Ops:
  0.7 23.2 %copy-start.5 = (s32[2]{0:T(128)S(1)}, s32[2]{0:T(128)}, u32[]{:S(2)}) copy-start(s32[2]{0:T(128)} %slices.3) | copy-start | bytes 28
  0.7 23.2 %copy-start.6 = (s32[2]{0:T(128)S(1)}, s32[2]{0:T(128)}, u32[]{:S(2)}) copy-start(s32[2]{0:T(128)} %moments.3) | copy-start | bytes 28
  7.6 16.6 %copy-start.3 = (f32[384,256]{1,0:T(8,128)S(1)}, f32[384,256]{1,0:T(8,128)}, u32[]{:S(2)}) copy-start(f32[384,256]{1,0:T(8,128)} %get-tuple-element.36.kept) | copy-start | bytes 1179652
  7.6 16.1 %collective-permute-start = (bf16[400,256]{1,0:T(8,128)(2,1)}, bf16[400,256]{1,0:T(8,128)(2,1)S(1)}, u32[]{:S(2)}, u32[]{:S(2)}) collective-permute-start(bf16[400,256]{1,0:T(8,128)(2,1)} %get-tuple-element.33), channel_id=1, source_target_pairs={{0,64},{16,80},{32,96},{48,112},{64,0},{80,16},{96,32},{112,48},{1... | collective-permute-start | bytes 614408 | tf_op jit(solution)/shard_map/ppermute | solution.py:387
  9.2 14.7 %collective-permute-start.1 = (bf16[400,256]{1,0:T(8,128)(2,1)}, bf16[400,256]{1,0:T(8,128)(2,1)S(1)}, u32[]{:S(2)}, u32[]{:S(2)}) collective-permute-start(bf16[400,256]{1,0:T(8,128)(2,1)} %get-tuple-element.34), channel_id=1, source_target_pairs={{0,128},{16,144},{32,160},{48,176},{64,192},{80,208},{96,224},{112... | collective-permute-start | bytes 614408 | tf_op jit(solution)/shard_map/ppermute | solution.py:387
  12.1 12.1 %collective-permute-start.2 = (bf16[400,256]{1,0:T(8,128)(2,1)}, bf16[400,256]{1,0:T(8,128)(2,1)S(1)}, u32[]{:S(2)}, u32[]{:S(2)}) collective-permute-start(bf16[400,256]{1,0:T(8,128)(2,1)} %get-tuple-element.35), channel_id=1, source_target_pairs={{0,192},{16,208},{32,224},{48,240},{64,128},{80,144},{96,160},{112... | collective-permute-start | bytes 614408 | tf_op jit(solution)/shard_map/ppermute | solution.py:387
  19.1 8.8 %collective-permute-start.6 = (bf16[400,256]{1,0:T(8,128)(2,1)}, bf16[400,256]{1,0:T(8,128)(2,1)S(1)}, u32[]{:S(2)}, u32[]{:S(2)}) collective-permute-start(bf16[400,256]{1,0:T(8,128)(2,1)} %get-tuple-element.42), channel_id=1, source_target_pairs={{0,64},{16,80},{32,96},{48,112},{64,0},{80,16},{96,32},{112,48},{1... | collective-permute-start | bytes 614408 | tf_op jit(solution)/shard_map/ppermute | solution.py:387
  19.6 12.8 %collective-permute-start.7 = (bf16[400,256]{1,0:T(8,128)(2,1)}, bf16[400,256]{1,0:T(8,128)(2,1)S(1)}, u32[]{:S(2)}, u32[]{:S(2)}) collective-permute-start(bf16[400,256]{1,0:T(8,128)(2,1)} %get-tuple-element.43), channel_id=1, source_target_pairs={{0,128},{16,144},{32,160},{48,176},{64,192},{80,208},{96,224},{112... | collective-permute-start | bytes 614408 | tf_op jit(solution)/shard_map/ppermute | solution.py:387
  23.7 11.1 %collective-permute-start.8 = (bf16[400,256]{1,0:T(8,128)(2,1)}, bf16[400,256]{1,0:T(8,128)(2,1)S(1)}, u32[]{:S(2)}, u32[]{:S(2)}) collective-permute-start(bf16[400,256]{1,0:T(8,128)(2,1)} %get-tuple-element.44), channel_id=1, source_target_pairs={{0,192},{16,208},{32,224},{48,240},{64,128},{80,144},{96,160},{112... | collective-permute-start | bytes 614408 | tf_op jit(solution)/shard_map/ppermute | solution.py:387
  24.3 15.0 %collective-permute-start.3 = (bf16[96,256]{1,0:T(8,128)(2,1)S(1)}, bf16[96,256]{1,0:T(8,128)(2,1)S(1)}, u32[]{:S(2)}, u32[]{:S(2)}) collective-permute-start(bf16[96,256]{1,0:T(8,128)(2,1)S(1)} %get-tuple-element.38), channel_id=1, source_target_pairs={{0,16},{16,0},{32,48},{48,32},{64,80},{80,64},{96,112},{112,96},{1... | collective-permute-start | bytes 147464 | tf_op jit(solution)/shard_map/ppermute | solution.py:391
  26.1 13.2 %collective-permute-start.4 = (bf16[96,256]{1,0:T(8,128)(2,1)S(1)}, bf16[96,256]{1,0:T(8,128)(2,1)S(1)}, u32[]{:S(2)}, u32[]{:S(2)}) collective-permute-start(bf16[96,256]{1,0:T(8,128)(2,1)S(1)} %get-tuple-element.39), channel_id=1, source_target_pairs={{0,32},{16,48},{32,0},{48,16},{64,96},{80,112},{96,64},{112,80},{1... | collective-permute-start | bytes 147464 | tf_op jit(solution)/shard_map/ppermute | solution.py:391
  28.0 11.4 %collective-permute-start.5 = (bf16[96,256]{1,0:T(8,128)(2,1)S(1)}, bf16[96,256]{1,0:T(8,128)(2,1)S(1)}, u32[]{:S(2)}, u32[]{:S(2)}) collective-permute-start(bf16[96,256]{1,0:T(8,128)(2,1)S(1)} %get-tuple-element.40), channel_id=1, source_target_pairs={{0,48},{16,32},{32,16},{48,0},{64,112},{80,96},{96,80},{112,64},{1... | collective-permute-start | bytes 147464 | tf_op jit(solution)/shard_map/ppermute | solution.py:391
  35.9 24.1 %collective-permute-start.10 = (bf16[96,256]{1,0:T(8,128)(2,1)S(1)}, bf16[96,256]{1,0:T(8,128)(2,1)S(1)}, u32[]{:S(2)}, u32[]{:S(2)}) collective-permute-start(bf16[96,256]{1,0:T(8,128)(2,1)S(1)} %get-tuple-element.47), channel_id=1, source_target_pairs={{0,32},{16,48},{32,0},{48,16},{64,96},{80,112},{96,64},{112,80},{1... | collective-permute-start | bytes 147464 | tf_op jit(solution)/shard_map/ppermute | solution.py:391
  39.2 21.4 %collective-permute-start.11 = (bf16[96,256]{1,0:T(8,128)(2,1)S(1)}, bf16[96,256]{1,0:T(8,128)(2,1)S(1)}, u32[]{:S(2)}, u32[]{:S(2)}) collective-permute-start(bf16[96,256]{1,0:T(8,128)(2,1)S(1)} %get-tuple-element.48), channel_id=1, source_target_pairs={{0,48},{16,32},{32,16},{48,0},{64,112},{80,96},{96,80},{112,64},{1... | collective-permute-start | bytes 147464 | tf_op jit(solution)/shard_map/ppermute | solution.py:391
  39.4 5.9 %collective-permute-start.15 = (bf16[3,2,16,256]{3,2,1,0:T(8,128)(2,1)S(1)}, bf16[3,2,16,256]{3,2,1,0:T(8,128)(2,1)S(1)}, u32[]{:S(2)}, u32[]{:S(2)}) collective-permute-start(bf16[3,2,16,256]{3,2,1,0:T(8,128)(2,1)S(1)} %bitcast.20), channel_id=1, source_target_pairs={{0,6},{1,7},{2,4},{3,5},{4,2},{5,3},{6,0},{7,1},{8,14},{9,15},{10,... | collective-permute-start | bytes 147464 | tf_op jit(solution)/shard_map/ppermute | solution.py:412
  42.2 5.6 %collective-permute-start.16 = (bf16[3,2,16,256]{3,2,1,0:T(8,128)(2,1)S(1)}, bf16[3,2,16,256]{3,2,1,0:T(8,128)(2,1)S(1)}, u32[]{:S(2)}, u32[]{:S(2)}) collective-permute-start(bf16[3,2,16,256]{3,2,1,0:T(8,128)(2,1)S(1)} %bitcast.21), channel_id=1, source_target_pairs={{0,4},{1,5},{2,6},{3,7},{4,0},{5,1},{6,2},{7,3},{8,12},{9,13},{10,... | collective-permute-start | bytes 147464 | tf_op jit(solution)/shard_map/ppermute | solution.py:412
  43.0 4.8 %collective-permute-start.17 = (bf16[3,2,16,256]{3,2,1,0:T(8,128)(2,1)S(1)}, bf16[3,2,16,256]{3,2,1,0:T(8,128)(2,1)S(1)}, u32[]{:S(2)}, u32[]{:S(2)}) collective-permute-start(bf16[3,2,16,256]{3,2,1,0:T(8,128)(2,1)S(1)} %bitcast.22), channel_id=1, source_target_pairs={{0,2},{1,3},{2,0},{3,1},{4,6},{5,7},{6,4},{7,5},{8,10},{9,11},{10,... | collective-permute-start | bytes 147464 | tf_op jit(solution)/shard_map/ppermute | solution.py:412
  45.3 15.3 %collective-permute-start.9 = (bf16[96,256]{1,0:T(8,128)(2,1)S(1)}, bf16[96,256]{1,0:T(8,128)(2,1)S(1)}, u32[]{:S(2)}, u32[]{:S(2)}) collective-permute-start(bf16[96,256]{1,0:T(8,128)(2,1)S(1)} %get-tuple-element.46), channel_id=1, source_target_pairs={{0,16},{16,0},{32,48},{48,32},{64,80},{80,64},{96,112},{112,96},{1... | collective-permute-start | bytes 147464 | tf_op jit(solution)/shard_map/ppermute | solution.py:391
  47.9 7.8 %collective-permute-start.18 = (bf16[3,2,16,256]{3,2,1,0:T(8,128)(2,1)S(1)}, bf16[3,2,16,256]{3,2,1,0:T(8,128)(2,1)S(1)}, u32[]{:S(2)}, u32[]{:S(2)}) collective-permute-start(bf16[3,2,16,256]{3,2,1,0:T(8,128)(2,1)S(1)} %select_select_fusion), channel_id=1, source_target_pairs={{0,40},{1,41},{2,42},{3,43},{4,44},{5,45},{6,46},{7,47},{8,32},{9,... | collective-permute-start | bytes 147464 | tf_op jit(solution)/shard_map/ppermute | solution.py:414
  55.7 1.3 %collective-permute-start.19 = (bf16[3,2,16,256]{3,2,1,0:T(8,128)(2,1)S(1)}, bf16[3,2,16,256]{3,2,1,0:T(8,128)(2,1)S(1)}, u32[]{:S(2)}, u32[]{:S(2)}) collective-permute-start(bf16[3,2,16,256]{3,2,1,0:T(8,128)(2,1)S(1)} %broadcast_select_fusion), channel_id=1, source_target_pairs={{0,1},{1,0},{2,3},{3,2},{4,5},{5,4},{6,7},{7,6},{8,9},{9,8},{10,11... | collective-permute-start | bytes 147464 | tf_op jit(solution)/shard_map/ppermute | solution.py:416
  57.0 4.6 %collective-permute-start.20 = (bf16[3,2,16,256]{3,2,1,0:T(8,128)(2,1)S(1)}, bf16[3,2,16,256]{3,2,1,0:T(8,128)(2,1)S(1)}, u32[]{:S(2)}, u32[]{:S(2)}) collective-permute-start(bf16[3,2,16,256]{3,2,1,0:T(8,128)(2,1)S(1)} %broadcast_select_fusion.1.p0), channel_id=1, source_target_pairs={{0,16},{16,0},{32,48},{48,32},{64,80},{80,64},{96,112},{112,96},{1... | collective-permute-start | bytes 147464 | tf_op jit(solution)/shard_map/ppermute | solution.py:391
  57.2 6.1 %collective-permute-start.21 = (bf16[3,2,16,256]{3,2,1,0:T(8,128)(2,1)S(1)}, bf16[3,2,16,256]{3,2,1,0:T(8,128)(2,1)S(1)}, u32[]{:S(2)}, u32[]{:S(2)}) collective-permute-start(bf16[3,2,16,256]{3,2,1,0:T(8,128)(2,1)S(1)} %broadcast_select_fusion.1.p0), channel_id=1, source_target_pairs={{0,32},{16,48},{32,0},{48,16},{64,96},{80,112},{96,64},{112,80},{1... | collective-permute-start | bytes 147464 | tf_op jit(solution)/shard_map/ppermute | solution.py:391
  59.9 5.3 %collective-permute-start.22 = (bf16[3,2,16,256]{3,2,1,0:T(8,128)(2,1)S(1)}, bf16[3,2,16,256]{3,2,1,0:T(8,128)(2,1)S(1)}, u32[]{:S(2)}, u32[]{:S(2)}) collective-permute-start(bf16[3,2,16,256]{3,2,1,0:T(8,128)(2,1)S(1)} %broadcast_select_fusion.1.p0), channel_id=1, source_target_pairs={{0,48},{16,32},{32,16},{48,0},{64,112},{80,96},{96,80},{112,64},{1... | collective-permute-start | bytes 147464 | tf_op jit(solution)/shard_map/ppermute | solution.py:391
  65.9 14.5 %collective-permute-start.26 = (bf16[2,4,2,16,256]{4,3,2,1,0:T(8,128)(2,1)S(1)}, bf16[2,4,2,16,256]{4,3,2,1,0:T(8,128)(2,1)S(1)}, u32[]{:S(2)}, u32[]{:S(2)}) collective-permute-start(bf16[2,4,2,16,256]{4,3,2,1,0:T(8,128)(2,1)S(1)} %get-tuple-element.50), channel_id=1, source_target_pairs={{0,64},{16,80},{32,96},{48,112},{64,0},{80,16},{96,32},{112,48},{1... | collective-permute-start | bytes 393224 | tf_op jit(solution)/shard_map/ppermute | solution.py:387
  66.0 5.8 %collective-permute-start.12 = (bf16[6,2,16,256]{3,2,1,0:T(8,128)(2,1)S(1)}, bf16[6,2,16,256]{3,2,1,0:T(8,128)(2,1)S(1)}, u32[]{:S(2)}, u32[]{:S(2)}) collective-permute-start(bf16[6,2,16,256]{3,2,1,0:T(8,128)(2,1)S(1)} %pad_maximum_fusion.p0), channel_id=1, source_target_pairs={{0,16},{16,0},{32,48},{48,32},{64,80},{80,64},{96,112},{112,96},{1... | collective-permute-start | bytes 294920 | tf_op jit(solution)/shard_map/ppermute | solution.py:391
  67.0 8.2 %collective-permute-start.13 = (bf16[6,2,16,256]{3,2,1,0:T(8,128)(2,1)S(1)}, bf16[6,2,16,256]{3,2,1,0:T(8,128)(2,1)S(1)}, u32[]{:S(2)}, u32[]{:S(2)}) collective-permute-start(bf16[6,2,16,256]{3,2,1,0:T(8,128)(2,1)S(1)} %pad_maximum_fusion.p0), channel_id=1, source_target_pairs={{0,32},{16,48},{32,0},{48,16},{64,96},{80,112},{96,64},{112,80},{1... | collective-permute-start | bytes 294920 | tf_op jit(solution)/shard_map/ppermute | solution.py:391
  68.8 9.1 %collective-permute-start.14 = (bf16[6,2,16,256]{3,2,1,0:T(8,128)(2,1)S(1)}, bf16[6,2,16,256]{3,2,1,0:T(8,128)(2,1)S(1)}, u32[]{:S(2)}, u32[]{:S(2)}) collective-permute-start(bf16[6,2,16,256]{3,2,1,0:T(8,128)(2,1)S(1)} %pad_maximum_fusion.p0), channel_id=1, source_target_pairs={{0,48},{16,32},{32,16},{48,0},{64,112},{80,96},{96,80},{112,64},{1... | collective-permute-start | bytes 294920 | tf_op jit(solution)/shard_map/ppermute | solution.py:391
  69.6 18.1 %collective-permute-start.27 = (bf16[2,4,2,16,256]{4,3,2,1,0:T(8,128)(2,1)S(1)}, bf16[2,4,2,16,256]{4,3,2,1,0:T(8,128)(2,1)S(1)}, u32[]{:S(2)}, u32[]{:S(2)}) collective-permute-start(bf16[2,4,2,16,256]{4,3,2,1,0:T(8,128)(2,1)S(1)} %get-tuple-element.51), channel_id=1, source_target_pairs={{0,128},{16,144},{32,160},{48,176},{64,192},{80,208},{96,224},{112... | collective-permute-start | bytes 393224 | tf_op jit(solution)/shard_map/ppermute | solution.py:387
  71.8 16.0 %collective-permute-start.28 = (bf16[2,4,2,16,256]{4,3,2,1,0:T(8,128)(2,1)S(1)}, bf16[2,4,2,16,256]{4,3,2,1,0:T(8,128)(2,1)S(1)}, u32[]{:S(2)}, u32[]{:S(2)}) collective-permute-start(bf16[2,4,2,16,256]{4,3,2,1,0:T(8,128)(2,1)S(1)} %get-tuple-element.52), channel_id=1, source_target_pairs={{0,192},{16,208},{32,224},{48,240},{64,128},{80,144},{96,160},{112... | collective-permute-start | bytes 393224 | tf_op jit(solution)/shard_map/ppermute | solution.py:387
  78.5 16.2 %collective-permute-start.23 = (bf16[2,4,2,16,256]{4,3,2,1,0:T(8,128)(2,1)S(1)}, bf16[2,4,2,16,256]{4,3,2,1,0:T(8,128)(2,1)S(1)}, u32[]{:S(2)}, u32[]{:S(2)}) collective-permute-start(bf16[2,4,2,16,256]{4,3,2,1,0:T(8,128)(2,1)S(1)} %get-tuple-element.58), channel_id=1, source_target_pairs={{0,64},{16,80},{32,96},{48,112},{64,0},{80,16},{96,32},{112,48},{1... | collective-permute-start | bytes 393224 | tf_op jit(solution)/shard_map/ppermute | solution.py:387
  80.3 14.4 %collective-permute-start.24 = (bf16[2,4,2,16,256]{4,3,2,1,0:T(8,128)(2,1)S(1)}, bf16[2,4,2,16,256]{4,3,2,1,0:T(8,128)(2,1)S(1)}, u32[]{:S(2)}, u32[]{:S(2)}) collective-permute-start(bf16[2,4,2,16,256]{4,3,2,1,0:T(8,128)(2,1)S(1)} %get-tuple-element.59), channel_id=1, source_target_pairs={{0,128},{16,144},{32,160},{48,176},{64,192},{80,208},{96,224},{112... | collective-permute-start | bytes 393224 | tf_op jit(solution)/shard_map/ppermute | solution.py:387
  80.4 14.3 %collective-permute-start.25 = (bf16[2,4,2,16,256]{4,3,2,1,0:T(8,128)(2,1)S(1)}, bf16[2,4,2,16,256]{4,3,2,1,0:T(8,128)(2,1)S(1)}, u32[]{:S(2)}, u32[]{:S(2)}) collective-permute-start(bf16[2,4,2,16,256]{4,3,2,1,0:T(8,128)(2,1)S(1)} %get-tuple-element.60), channel_id=1, source_target_pairs={{0,192},{16,208},{32,224},{48,240},{64,128},{80,144},{96,160},{112... | collective-permute-start | bytes 393224 | tf_op jit(solution)/shard_map/ppermute | solution.py:387
  (4 other events, 12.5 us)
